TPU v7x, 128 devices: a whole 4x4x4 slice. The times are simulated.
128 devices in a mesh: exp: 16 (over x, z), sky: 8 (over y, core).
Axes of the slice: x: 4, y: 4, z: 4, core: 2. Of those that a mesh axis runs over, the one named last changes fastest.
Arguments:
- image: float32 [16, 4096, 4096], P('exp', 'sky'), may hold values from -21 to 21
- variance: float32 [16, 4096, 4096], P('exp', 'sky'), may hold values from 0.25 to 4
- mask: int32 [16, 256, 256], P('exp', 'sky'), may hold values 0 or 1
- foot_start: int32 [16], replicated, may hold values from 0 to 64
- pair_owner: int32 [16, 16], replicated, may hold values from 0 to 1, as said below
Outputs:
- coadd: float32 [4096, 4096], P('sky', 'exp')
- offsets: float32 [16, 9], replicated
Inputs may be any that keep to these rules, and one draw needn't show every extreme that they name: pair_owner is 0 or 1, zero on the diagonal, pair_owner[i, j] and pair_owner[j, i] are never both 1, and every exposure has at least one pair.
All inputs are finite; a program needn't handle non-finite values. No bound on the sum of `mask` on one device may be relied on, other than what follows from the above.
Results may differ from a plain program's by a relative error of at most 0.0003.
Values sent between devices are 32-bit elements; how exact they have to be, the bound alone decides.
A program may use at most 256 MiB of HBM per device.

v0:
```python
import functools

import jax
import jax.numpy as jnp
import numpy as np
from jax import lax
from jax.experimental import pallas as pl
from jax.experimental.pallas import tpu as pltpu
from jax.sharding import PartitionSpec as P

F32 = jnp.float32
BF16 = jnp.bfloat16
HIGH = lax.Precision.HIGHEST
MESH = pl.DeviceIdType.MESH
BIN = 16
RADIUS = 10
NEXP = 16
ROWS = 512
COLS = 4096
SKY = 8
BROWS = 32
BCOLS = 256
FOOT_BINS = 192
HALO = 16
LAMBDA_REG = 0.25
PRIOR = 1.0


def iota(shape, dim):
    return lax.broadcasted_iota(jnp.int32, shape, dim)


def center(index, total):
    return (2.0 * index.astype(F32) + 1.0) / total - 1.0


def cheb(order, t):
    if order == 0:
        return jnp.ones_like(t)
    if order == 1:
        return t
    return 2.0 * t * t - 1.0


def split(value):
    high = value.astype(BF16)
    return high, (value - high.astype(F32)).astype(BF16)


def weigh_kernel(foot_ref, image_ref, variance_ref, mask_ref, weight_ref, bins_ref, sums, ones):
    step = pl.program_id(0)
    rows = image_ref.shape[1]
    start = foot_ref[lax.axis_index("exp")]

    @pl.when(step == 0)
    def _():
        hit = (iota((2048, 128), 0) // BIN) == iota((2048, 128), 1)
        ones[...] = jnp.where(hit, 1.0, 0.0).astype(BF16)

    nb = rows // BIN
    blocks = mask_ref[0, pl.ds(pl.multiple_of((step // 2) * 8, 8), 8), :].astype(F32)
    odd = (step % 2) == 1
    blocks = jnp.where(odd, blocks[nb:], blocks[:nb])
    cell = iota((nb, BCOLS), 1)
    blocks = jnp.where((cell >= start) & (cell < start + FOOT_BINS), blocks, 0.0)
    eight = jnp.concatenate([blocks, blocks], 0)
    lane = iota((8, 128), 1) // BIN
    wsums, isums = [], []
    for m in range(16):
        tiles = []
        for t in (2 * m, 2 * m + 1):
            half = eight[:, 128 * (t // 16) : 128 * (t // 16) + 128]
            tiles.append(jnp.take_along_axis(half, lane + 8 * (t % 16), axis=1))
        wide = jnp.concatenate(tiles, 1)[:nb]
        wide = jnp.broadcast_to(wide[:, None, :], (nb, BIN, 256)).reshape(rows, 256)
        w = wide * (1.0 / variance_ref[0, :, 256 * m : 256 * m + 256])
        weight_ref[m] = w
        wsums.append(jnp.sum(w.reshape(nb, BIN, 256), axis=1))
        isums.append(jnp.sum(image_ref[0, :, 256 * m : 256 * m + 256].reshape(nb, BIN, 256), axis=1))
    wsum = jnp.concatenate(wsums, 1)
    isum = jnp.concatenate(isums, 1) * (1.0 / (BIN * BIN))
    zero = jnp.zeros((4, COLS), F32)
    for k in range(nb // 2):
        tile = jnp.concatenate([isum[2 * k : 2 * k + 2], wsum[2 * k : 2 * k + 2], zero], 0)
        sums[pl.ds(pl.multiple_of(8 * (step * (nb // 2) + k), 8), 8), :] = tile

    @pl.when(step == pl.num_programs(0) - 1)
    def _():
        for h in range(2):
            x = sums[:, 2048 * h : 2048 * h + 2048]
            high = x.astype(BF16)
            rest = x - high.astype(F32)
            mid = rest.astype(BF16)
            low = (rest - mid.astype(F32)).astype(BF16)
            got = jnp.dot(jnp.concatenate([high, mid, low], 0), ones[...], preferred_element_type=F32)
            got = got[:128] + got[128:256] + got[256:]
            bins_ref[:, :, 128 * h : 128 * h + 128] = got.reshape(16, 8, 128)


def weigh(image, variance, mask, foot_start):
    rows = 64
    return pl.pallas_call(
        weigh_kernel,
        grid=(ROWS // rows,),
        in_specs=[
            pl.BlockSpec(memory_space=pltpu.SMEM),
            pl.BlockSpec((1, rows, COLS), lambda i: (0, i, 0)),
            pl.BlockSpec((1, rows, COLS), lambda i: (0, i, 0)),
            pl.BlockSpec((1, BROWS, BCOLS), lambda i: (0, 0, 0)),
        ],
        out_specs=[
            pl.BlockSpec((16, rows, 256), lambda i: (0, i, 0)),
            pl.BlockSpec((16, 8, BCOLS), lambda i: (0, 0, 0)),
        ],
        out_shape=[
            jax.ShapeDtypeStruct((16, ROWS, 256), F32),
            jax.ShapeDtypeStruct((16, 8, BCOLS), F32),
        ],
        scratch_shapes=[pltpu.VMEM((128, COLS), F32), pltpu.VMEM((2048, 128), BF16)],
        compiler_params=pltpu.CompilerParams(vmem_limit_bytes=40 << 20),
        cost_estimate=pl.CostEstimate(flops=10**8, bytes_accessed=25 << 20, transcendentals=2 << 20),
        name="weigh",
    )(foot_start, image, variance, mask)


def taps_matrix(offset):
    total = np.sum(np.exp(-(np.arange(-RADIUS, RADIUS + 1) ** 2) / 50.0))
    exact = np.where(np.abs(offset) <= RADIUS, np.exp(-(offset**2) / 50.0) / total, 0.0)
    high = exact.astype(BF16)
    return jnp.asarray(high), jnp.asarray((exact - high.astype(np.float64)).astype(BF16))


def smooth_kernel(foot_ref, up_ref, down_ref, prev_ref, image_ref, next_ref, ch_ref, cl_ref, rh_ref, rl_ref,
                  smooth_ref, tx_ref, ty_ref, xh, xl):
    j = pl.program_id(0)
    band = lax.axis_index("sky")
    start = foot_ref[lax.axis_index("exp")] * BIN
    tall = ROWS + 2 * HALO

    def put(first, lane0, value):
        rows, width = value.shape
        col = 256 * j - 128 + lane0 + iota((1, width), 1)
        inside = (col >= start) & (col < start + FOOT_BINS * BIN)
        high, low = split(jnp.where(inside, value, 0.0))
        xh[first : first + rows, lane0 : lane0 + width] = high
        xl[first : first + rows, lane0 : lane0 + width] = low

    lo = pl.multiple_of(jnp.maximum(256 * j - 128, 0), 128)
    mid = pl.multiple_of(256 * j, 128)
    hi = pl.multiple_of(jnp.minimum(256 * j + 256, COLS - 128), 128)
    for first, ref in ((0, up_ref), (HALO + ROWS, down_ref)):
        put(first, 0, ref[:, pl.ds(lo, 128)])
        put(first, 128, ref[:, pl.ds(mid, 256)])
        put(first, 384, ref[:, pl.ds(hi, 128)])
    put(HALO, 0, prev_ref[0])
    put(HALO, 128, image_ref[0])
    put(HALO, 384, next_ref[0])
    xcol = center(256 * j - 128 + iota((16, 512), 1), COLS)
    order = iota((16, 512), 0)
    put(tall, 0, jnp.where(order == 0, 1.0, jnp.where(order == 1, xcol, 2.0 * xcol * xcol - 1.0)))

    def row_pass(value):
        high, low = split(value)
        parts = []
        for i in range(ROWS // 128):
            zh, zl = high[128 * i : 128 * i + 160], low[128 * i : 128 * i + 160]
            parts.append(
                jnp.dot(rh_ref[...], zh, preferred_element_type=F32)
                + jnp.dot(rl_ref[...], zh, preferred_element_type=F32)
                + jnp.dot(rh_ref[...], zl, preferred_element_type=F32)
            )
        return parts

    across = (
        jnp.dot(xh[...], ch_ref[...], preferred_element_type=F32)
        + jnp.dot(xl[...], ch_ref[...], preferred_element_type=F32)
        + jnp.dot(xh[...], cl_ref[...], preferred_element_type=F32)
    )
    tx_ref[...] = across[tall : tall + 8]
    for i, part in enumerate(row_pass(across[:tall])):
        smooth_ref[0, 128 * i : 128 * i + 128, :] = part

    @pl.when(j == 0)
    def _():
        row = band * ROWS - HALO + iota((tall, 128), 0)
        y = center(row, ROWS * SKY)
        known = (row >= 0) & (row < ROWS * SKY)
        for u in range(3):
            for i, part in enumerate(row_pass(jnp.where(known, cheb(u, y), 0.0))):
                ty_ref[u, 128 * i : 128 * i + 128, :] = part


def smooth(image, up, down, foot_start):
    k, n = np.arange(512)[:, None], np.arange(256)[None, :]
    ch, cl = taps_matrix(k - n - 128)
    k, n = np.arange(160)[None, :], np.arange(128)[:, None]
    rh, rl = taps_matrix(k - n - HALO)
    last = COLS // 128 - 1
    whole = lambda shape: pl.BlockSpec(shape, lambda j: (0, 0))
    return pl.pallas_call(
        smooth_kernel,
        grid=(16,),
        in_specs=[
            pl.BlockSpec(memory_space=pltpu.SMEM),
            whole((HALO, COLS)),
            whole((HALO, COLS)),
            pl.BlockSpec((1, ROWS, 128), lambda j: (0, 0, jnp.maximum(2 * j - 1, 0))),
            pl.BlockSpec((1, ROWS, 256), lambda j: (0, 0, j)),
            pl.BlockSpec((1, ROWS, 128), lambda j: (0, 0, jnp.minimum(2 * j + 2, last))),
            whole((512, 256)),
            whole((512, 256)),
            whole((128, 160)),
            whole((128, 160)),
        ],
        out_specs=[
            pl.BlockSpec((1, ROWS, 256), lambda j: (j, 0, 0)),
            pl.BlockSpec((8, 256), lambda j: (0, j)),
            pl.BlockSpec((3, ROWS, 128), lambda j: (0, 0, 0)),
        ],
        out_shape=[
            jax.ShapeDtypeStruct((16, ROWS, 256), F32),
            jax.ShapeDtypeStruct((8, COLS), F32),
            jax.ShapeDtypeStruct((3, ROWS, 128), F32),
        ],
        scratch_shapes=[pltpu.VMEM((ROWS + 2 * HALO + 16, 512), BF16)] * 2,
        compiler_params=pltpu.CompilerParams(vmem_limit_bytes=40 << 20),
        cost_estimate=pl.CostEstimate(flops=10**10, bytes_accessed=25 << 20, transcendentals=0),
        name="smooth",
    )(foot_start, up, down, image, image, image, ch, cl, rh, rl)


def add_into(dst, terms, blocks, rows):
    per = rows // 64

    def body(i, carry):
        b, r = i // per, pl.multiple_of((i % per) * 64, 64)
        total = terms[0](b, r)
        for term in terms[1:]:
            total = total + term(b, r)
        dst(b, r, total)
        return carry

    lax.fori_loop(0, blocks * per, body, 0)


class Scatter:
    def __init__(self, part, half, x, z, sky, bufs, sems, first_sem):
        self.part, self.half = part, half
        self.me = (x, z)
        self.sky = sky
        self.f1p, self.f1m, self.rp, self.rm, self.f2p, self.f2m, self.r2p, self.r2m = bufs
        self.send_sems, self.recv_sems = sems
        self.sem = first_sem
        self.row0 = 256 * half
        self.lead = half
        self.copies = {}

    def device(self, axis, shift):
        x, z = self.me
        if axis == 0:
            x = lax.rem(x + shift + 4, 4)
        else:
            z = lax.rem(z + shift + 4, 4)
        return (4 * x + z, self.sky)

    def group(self, ref, dist, r, rows):
        g = lax.rem(self.me[self.lead] + dist, 4)
        rows = pl.ds(self.row0 + r, rows)
        return ref.at[g, :, rows, :] if self.lead == 0 else ref.at[:, g, rows, :]

    def send(self, key, src, dst, axis, shift):
        n = self.sem
        self.sem += 1
        copy = pltpu.make_async_remote_copy(
            src_ref=src, dst_ref=dst, send_sem=self.send_sems.at[n], recv_sem=self.recv_sems.at[n],
            device_id=self.device(axis, shift), device_id_type=MESH,
        )
        copy.start()
        self.copies[key] = copy

    def start1(self, ref):
        self.send("1p", self.group(ref, 2, 0, 128), self.f1p, self.lead, 1)
        self.send("1m", self.group(ref, 2, 128, 128), self.f1m, self.lead, -1)

    def start2(self, ref):
        self.send("2p", self.group(ref, 1, 128, 128), self.rp.at[:, pl.ds(128, 128), :], self.lead, 1)
        self.send("2m", self.group(ref, 3, 0, 128), self.rm.at[:, pl.ds(0, 128), :], self.lead, -1)

    def load(self, dist, shift):
        g = lax.rem(self.me[self.lead] + dist, 4)

        def get(b, r):
            rows = pl.ds(self.row0 + shift + r, 64)
            return self.part[g, b, rows, :] if self.lead == 0 else self.part[b, g, rows, :]

        return get

    def start3(self):
        for key, buf, dist, shift, to in (("p", self.f1p, 1, 0, 1), ("m", self.f1m, 3, 128, -1)):
            self.copies["1" + key].wait_recv()

            def put(b, r, v, buf=buf):
                buf[b, pl.ds(r, 64), :] = v

            add_into(put, [lambda b, r, buf=buf: buf[b, pl.ds(r, 64), :], self.load(dist, shift)], 4, 128)
            land = self.rp if to == 1 else self.rm
            self.send("3" + key, buf, land.at[:, pl.ds(shift, 128), :], self.lead, to)

    def finish1(self):
        for key in ("2p", "2m", "3p", "3m"):
            self.copies[key].wait_recv()

        def put(b, r, v):
            self.rp[b, pl.ds(r, 64), :] = v

        add_into(
            put,
            [lambda b, r: self.rp[b, pl.ds(r, 64), :], lambda b, r: self.rm[b, pl.ds(r, 64), :], self.load(0, 0)],
            4, 256,
        )
        axis = 1 - self.lead
        at = lambda dist: lax.rem(self.me[axis] + dist, 4)
        top, low = pl.ds(0, 128), pl.ds(128, 128)
        self.send("4p", self.rp.at[at(2), top, :], self.f2p, axis, 1)
        self.send("4m", self.rp.at[at(2), low, :], self.f2m, axis, -1)
        self.send("5p", self.rp.at[at(1), low, :], self.r2p.at[low, :], axis, 1)
        self.send("5m", self.rp.at[at(3), top, :], self.r2m.at[top, :], axis, -1)

    def start6(self):
        axis = 1 - self.lead
        for key, buf, dist, shift, to in (("p", self.f2p, 1, 0, 1), ("m", self.f2m, 3, 128, -1)):
            self.copies["4" + key].wait_recv()
            g = lax.rem(self.me[axis] + dist, 4)

            def put(b, r, v, buf=buf):
                buf[pl.ds(r, 64), :] = v

            add_into(
                put,
                [lambda b, r, buf=buf: buf[pl.ds(r, 64), :],
                 lambda b, r, g=g, shift=shift: self.rp[g, pl.ds(shift + r, 64), :]],
                1, 128,
            )
            land = self.r2p if to == 1 else self.r2m
            self.send("6" + key, buf, land.at[pl.ds(shift, 128), :], axis, to)

    def finish2(self):
        for key in ("5p", "5m", "6p", "6m"):
            self.copies[key].wait_recv()

    def total(self, r):
        g = self.me[1 - self.lead]
        return self.rp[g, pl.ds(r, 64), :] + self.r2p[pl.ds(r, 64), :] + self.r2m[pl.ds(r, 64), :]

    def drain(self):
        for copy in self.copies.values():
            copy.wait_send()


def invert(system):
    lane, row = iota((NEXP, 128), 1), iota((NEXP, 128), 0)
    work = jnp.concatenate([system, jnp.zeros((NEXP, 112), F32)], 1)
    work = work + jnp.where(lane == row + NEXP, 1.0, 0.0)
    for j in range(NEXP):
        pivot_row = work[j : j + 1, :] / work[j : j + 1, j : j + 1]
        factor = work[:, j : j + 1]
        work = jnp.where(row == j, pivot_row, work - factor * pivot_row)
    return work[:, NEXP : 2 * NEXP]


def moments(bins, me, band):
    image = jnp.concatenate([bins[:, 0, :], bins[:, 1, :]], 1)
    weight = jnp.concatenate([bins[:, 2, :], bins[:, 3, :]], 1)
    ws, ds = [], []
    for d in range(1, 9):
        other = pltpu.roll(weight, NEXP - d, 0)
        w = weight * other / (weight + other + 1.0)
        ws.append(w)
        ds.append(w * (image - pltpu.roll(image, NEXP - d, 0)))
    w, wd = jnp.concatenate(ws, 0), jnp.concatenate(ds, 0)

    def basis(rows, base):
        k, lane = iota((rows, 512), 0), iota((rows, 512), 1)
        y = center(BROWS * band + 2 * me + lane // 256, BCOLS)
        x = center(lane % 256, BCOLS)

        def pick(order, t):
            t2 = 2.0 * t * t - 1.0
            out = jnp.where(order == 0, 1.0, jnp.where(order == 1, t, t2))
            if base == 5:
                out = jnp.where(order == 3, 2.0 * t * t2 - t, out)
                out = jnp.where(order == 4, 2.0 * t2 * t2 - 1.0, out)
            return out

        return jnp.where(k < base * base, pick(k // base, y) * pick(k % base, x), 0.0)

    nt = (((1,), (1,)), ((), ()))
    gram = lax.dot_general(basis(32, 5), w, nt, precision=HIGH, preferred_element_type=F32)
    rhs = lax.dot_general(basis(16, 3), wd, nt, precision=HIGH, preferred_element_type=F32)
    return jnp.concatenate([gram, rhs], 0)


def solve_lanes(mom):
    m = lambda a, b: mom[5 * a + b : 5 * a + b + 1, :]
    cache = {}

    def entry(k, l):
        u, v, s, t = k // 3, k % 3, l // 3, l % 3
        key = tuple(sorted(((u + s, v + t), (abs(u - s), v + t), (u + s, abs(v - t)), (abs(u - s), abs(v - t)))))
        if key not in cache:
            cache[key] = 0.25 * ((m(*key[0]) + m(*key[1])) + (m(*key[2]) + m(*key[3])))
        return cache[key]

    a = [[entry(k, l) for l in range(k + 1)] for k in range(9)]
    b = [mom[32 + k : 33 + k, :] for k in range(9)]
    inv = [None] * 9
    for j in range(9):
        inv[j] = 1.0 / a[j][j]
        for k in range(j + 1, 9):
            f = a[k][j] * inv[j]
            for l in range(j + 1, k + 1):
                a[k][l] = a[k][l] - f * a[l][j]
            b[k] = b[k] - f * b[j]
    out = [None] * 9
    for j in reversed(range(9)):
        total = b[j]
        for k in range(j + 1, 9):
            total = total - a[k][j] * out[k]
        out[j] = total * inv[j]
    return out


def coadd_kernel(bins_ref, owner_ref, tx_ref, ty_ref, weight_hbm, smooth_hbm, coadd_ref, offsets_ref, *scratch):
    (wv, sv, bins, mom, sky_mom, exp_mom, offs, px), scratch = scratch[:8], scratch[8:]
    bufs, scratch = scratch[:32], scratch[32:]
    load_sems, send_sems, recv_sems, bin_s, bin_r, sky_s, sky_r, exp_s, exp_r = scratch
    me, band = lax.axis_index("exp"), lax.axis_index("sky")
    x, z = me // 4, lax.rem(me, 4)

    barrier = pltpu.get_barrier_semaphore()
    for k in range(1, NEXP):
        pl.semaphore_signal(barrier, inc=1, device_id=(lax.rem(me + k, NEXP), band), device_id_type=MESH)
    for k in range(1, SKY):
        pl.semaphore_signal(barrier, inc=1, device_id=(me, lax.rem(band + k, SKY)), device_id_type=MESH)
    load_w = pltpu.make_async_copy(weight_hbm, wv, load_sems.at[0])
    load_s = pltpu.make_async_copy(smooth_hbm, sv, load_sems.at[1])
    load_w.start()
    load_s.start()
    pl.semaphore_wait(barrier, NEXP + SKY - 2)

    bin_copies = []
    for k in range(1, NEXP):
        to = lax.rem(me + k, NEXP)
        copy = pltpu.make_async_remote_copy(
            src_ref=bins_ref.at[to], dst_ref=bins.at[me], send_sem=bin_s.at[k], recv_sem=bin_r.at[k],
            device_id=(to, band), device_id_type=MESH,
        )
        copy.start()
        bin_copies.append(copy)
    make = lambda part, n: [
        Scatter(part, half, x, z, band, bufs[8 * (2 * n + half) : 8 * (2 * n + half) + 8],
                (send_sems, recv_sems), 12 * (2 * n + half))
        for half in range(2)
    ]
    den, num = make(wv, 0), make(sv, 1)
    for part in den:
        part.start1(weight_hbm)
    for part in den:
        part.start2(weight_hbm)

    bins[me] = bins_ref[me]
    owner = owner_ref[...].astype(F32)
    both = owner + owner.T
    eye = iota((NEXP, NEXP), 0) == iota((NEXP, NEXP), 1)
    degree = jnp.sum(both, axis=1, keepdims=True) + LAMBDA_REG
    inverse = invert(jnp.where(eye, degree, 0.0) - both)
    lane, row = iota((NEXP, 128), 1), iota((NEXP, 128), 0)
    first = lax.rem(lane, NEXP)
    shift = lane // NEXP + 1
    second = lax.rem(first + shift, NEXP)
    at_first, at_second = row == first, row == second
    partner = jnp.dot(both, jnp.where(at_second, 1.0, 0.0), precision=HIGH, preferred_element_type=F32)
    used = jnp.sum(jnp.where(at_first, partner, 0.0), axis=0, keepdims=True)
    used = jnp.where((shift[:1] == 8) & (first[:1] >= 8), 0.0, used)
    sign = jnp.where(at_first, 1.0, 0.0) - jnp.where(at_second, 1.0, 0.0)

    for copy in bin_copies:
        copy.wait_recv()
    own = moments(bins, me, band)
    mom[...] = own
    sky_mom[band] = own
    sky_copies = []
    for k in range(1, SKY):
        copy = pltpu.make_async_remote_copy(
            src_ref=mom, dst_ref=sky_mom.at[band], send_sem=sky_s.at[k], recv_sem=sky_r.at[k],
            device_id=(me, lax.rem(band + k, SKY)), device_id_type=MESH,
        )
        copy.start()
        sky_copies.append(copy)
    for copy in sky_copies:
        copy.wait()
    total = sky_mom[0]
    for k in range(1, SKY):
        total = total + sky_mom[k]
    mom[...] = total
    exp_mom[me] = total
    exp_copies = []
    for k in range(1, NEXP):
        copy = pltpu.make_async_remote_copy(
            src_ref=mom, dst_ref=exp_mom.at[me], send_sem=exp_s.at[k], recv_sem=exp_r.at[k],
            device_id=(lax.rem(me + k, NEXP), band), device_id_type=MESH,
        )
        copy.start()
        exp_copies.append(copy)

    load_w.wait()
    for part in den:
        part.start3()

    for copy in exp_copies:
        copy.wait()
    total = exp_mom[0]
    for k in range(1, NEXP):
        total = total + exp_mom[k]
    mom[...] = total
    fits = jnp.concatenate(solve_lanes(mom) + [jnp.zeros((7, 128), F32)], 0)
    fits = jnp.where(used > 0.0, fits, 0.0)
    nt = (((1,), (1,)), ((), ()))
    right = lax.dot_general(sign, fits, nt, precision=HIGH, preferred_element_type=F32)
    answer = jnp.dot(inverse, right, precision=HIGH, preferred_element_type=F32)
    offsets_ref[...] = answer[:, :9]
    offs[:, 0:NEXP] = answer
    coef = offs[pl.ds(me, 1), :]
    for u in range(3):
        line = coef[:, 3 * u : 3 * u + 1] * tx_ref[0:1, :]
        for v in range(1, 3):
            line = line + coef[:, 3 * u + v : 3 * u + v + 1] * tx_ref[v : v + 1, :]
        for m in range(16):
            px[m, u : u + 1, :] = line[:, 256 * m : 256 * m + 256]

    load_s.wait()

    def numerator(half, dist):
        lead = (x, z)[half]
        g = lax.rem(lead + dist, 4)

        def body(i, carry):
            b, r = i // 4, pl.multiple_of(256 * half + lax.rem(i, 4) * 64, 64)
            cx, cz = (g, b) if half == 0 else (b, g)
            rows = pl.ds(r, 64)
            back = None
            for u in range(3):
                ty = ty_ref[u, rows, :]
                term = jnp.concatenate([ty, ty], 1) * px[4 * cx + cz, u : u + 1, :]
                back = term if back is None else back + term
            sv[cx, cz, rows, :] = wv[cx, cz, rows, :] * (sv[cx, cz, rows, :] - back)
            return carry

        lax.fori_loop(0, 16, body, 0)

    for half in range(2):
        numerator(half, 2)
        num[half].start1(sv)
    for half in range(2):
        numerator(half, 1)
        numerator(half, 3)
        num[half].start2(sv)
    for half in range(2):
        numerator(half, 0)
    for part in den:
        part.finish1()
    for part in num:
        part.start3()
    for part in den:
        part.start6()
    for part in num:
        part.finish1()
    for part in den:
        part.finish2()
    for part in num:
        part.start6()
    for part in num:
        part.finish2()
    for half in range(2):

        def body(i, carry):
            r = pl.multiple_of(i * 64, 64)
            coadd_ref[pl.ds(256 * half + r, 64), :] = num[half].total(r) / (PRIOR + den[half].total(r))
            return carry

        lax.fori_loop(0, 4, body, 0)
    for copy in bin_copies:
        copy.wait_send()
    for part in den + num:
        part.drain()


def fit_and_sum(bins, owner, tx, ty, weight, smoothed):
    big = lambda *shape: pltpu.VMEM(shape, F32)
    set_of = [big(4, 128, 256), big(4, 128, 256), big(4, 256, 256), big(4, 256, 256),
              big(128, 256), big(128, 256), big(256, 256), big(256, 256)]
    vmem = pl.BlockSpec(memory_space=pltpu.VMEM)
    hbm = pl.BlockSpec(memory_space=pl.ANY)
    dma = lambda n: pltpu.SemaphoreType.DMA((n,))
    return pl.pallas_call(
        coadd_kernel,
        in_specs=[vmem, vmem, vmem, vmem, hbm, hbm],
        out_specs=[vmem, vmem],
        out_shape=[jax.ShapeDtypeStruct((ROWS, 256), F32), jax.ShapeDtypeStruct((NEXP, 9), F32)],
        scratch_shapes=[
            big(4, 4, ROWS, 256), big(4, 4, ROWS, 256), big(NEXP, 8, BCOLS), big(48, 128), big(SKY, 48, 128),
            big(NEXP, 48, 128), big(NEXP, 128), big(16, 8, 256),
        ] + set_of * 4 + [dma(2), dma(48), dma(48), dma(NEXP), dma(NEXP), dma(SKY), dma(SKY), dma(NEXP), dma(NEXP)],
        compiler_params=pltpu.CompilerParams(
            collective_id=0, has_side_effects=True, vmem_limit_bytes=48 << 20
        ),
        cost_estimate=pl.CostEstimate(flops=10**8, bytes_accessed=64 << 20, transcendentals=0),
        name="fit_and_sum",
    )(bins, owner, tx, ty, weight.reshape(4, 4, ROWS, 256), smoothed.reshape(4, 4, ROWS, 256))


def per_device(image, variance, mask, foot_start, pair_owner):
    up_pairs = [(i, i + 1) for i in range(SKY - 1)]
    up = lax.ppermute(image[0, ROWS - HALO :, :], "sky", up_pairs)
    down = lax.ppermute(image[0, :HALO, :], "sky", [(j, i) for i, j in up_pairs])
    weight, bins = weigh(image, variance, mask, foot_start)
    smoothed, tx, ty = smooth(image, up, down, foot_start)
    return tuple(fit_and_sum(bins, pair_owner, tx, ty, weight, smoothed))


def solution(mesh):
    placed = (P("exp", "sky", None), P("exp", "sky", None), P("exp", "sky", None), P(), P())
    return jax.shard_map(
        per_device, mesh=mesh, in_specs=placed, out_specs=(P("sky", "exp"), P()), check_vma=False
    )
```

profile of v0, /device:TPU:0, one launch (start us, length us, event | category | flops | bytes accessed | tf_op | source)
XLA Modules:
  0.0 151.5 jit_solution(6638459530068024606)
XLA Ops:
  0.6 1.1 slice_bitcast_fusion
  1.7 1.3 collective-permute-start.1
  3.0 3.0 %collective-permute-start = (f32[16,4096]{1,0:T(8,128)S(1)}, f32[16,4096]{1,0:T(8,128)S(1)}, u32[]{:S(2)}, u32[]{:S(2)}) collective-permute-start(f32[16,4096]{1,0:T(8,128)S(1)} %get-tuple-element.13), channel_id=1, source_target_pairs={{0,1},{1,2},{2,3},{3,4},{4,5},{5,6},{6,7},{8,9},{9,10},{10,11},{11... | collective-permute-start | bytes 786440 | tf_op jit(solution)/shard_map/ppermute | solution.py:624
  6.1 0.0 copy-start.2
  6.1 0.7 copy-done.2
  6.8 0.0 copy-start.4
  6.8 0.7 copy-done.4
  7.5 0.0 copy-start.5
  7.5 0.0 copy-start.6
  7.5 0.0 copy-start.7
  7.5 0.0 copy-start.8
  7.5 10.6 %weigh.1 = (f32[16,512,256]{2,1,0:T(8,128)S(1)}, f32[16,8,256]{2,1,0:T(8,128)S(1)}) custom-call(s32[16]{0:T(128)S(1)} %copy-done.4, f32[1,512,4096]{2,1,0:T(8,128)} %next_ref.1, f32[1,512,4096]{2,1,0:T(8,128)} %variance_ref.1, s32[1,32,256]{2,1,0:T(8,128)S(1)} %copy-done.2), custom_call_target="tpu_custom_call" | custom-call | flops 100000000 | bytes 26214400 | tf_op jit(solution)/shard_map/weigh/pallas_call | solution.py:102
  18.1 0.0 copy-start
  18.1 3.2 %copy-done = f32[16,512,256]{2,1,0:T(8,128)} copy-done((f32[16,512,256]{2,1,0:T(8,128)}, f32[16,512,256]{2,1,0:T(8,128)S(1)}, u32[]{:S(2)}) %copy-start) | copy-done | bytes 8388632
  21.3 0.0 copy-start.3
  21.3 0.0 collective-permute-done.1.down_ref
  21.3 0.0 collective-permute-done.up_ref
  21.3 0.0 copy-done.5
  21.4 0.0 copy-done.6
  21.4 0.0 copy-done.7
  21.4 0.0 copy-done.8
  21.4 23.3 %smooth.1 = (f32[16,512,256]{2,1,0:T(8,128)S(1)}, f32[8,4096]{1,0:T(8,128)S(1)}, f32[3,512,128]{2,1,0:T(8,128)S(1)}) custom-call(s32[16]{0:T(128)S(1)} %copy-done.4, f32[16,4096]{1,0:T(8,128)S(1)} %collective-permute-done.up_ref, f32[16,4096]{1,0:T(8,128)S(1)} %collective-permute-done.1.down_ref, f32[1,512,4096]{2,1,0:T(8,128)} %next_ref.1, ...), custom_call_target="tpu_custom_call" | custom-call | flops 10000000000 | bytes 26214400 | tf_op jit(solution)/shard_map/smooth/pallas_call | solution.py:200
  44.7 0.0 copy-start.1
  44.7 3.2 %copy-done.1 = f32[16,512,256]{2,1,0:T(8,128)} copy-done((f32[16,512,256]{2,1,0:T(8,128)}, f32[16,512,256]{2,1,0:T(8,128)S(1)}, u32[]{:S(2)}) %copy-start.1) | copy-done | bytes 8388632
  47.9 0.0 copy-done.3
  47.9 102.1 %fit_and_sum.1 = (f32[512,256]{1,0:T(8,128)S(1)}, f32[16,9]{1,0:T(8,128)S(1)}) custom-call(f32[16,8,256]{2,1,0:T(8,128)S(1)} %get-tuple-element.7.bins_ref, s32[16,16]{1,0:T(8,128)S(1)} %copy-done.3, f32[8,4096]{1,0:T(8,128)S(1)} %get-tuple-element.8.tx_ref, f32[3,512,128]{2,1,0:T(8,128)S(1)} %get-tuple-element.9.ty_ref, f32[4,4,512,256]{3,2,1,0:T(8,128)} %bitcast.6, ...), custom_call_target="tpu_custom_call" | custom-call | flops 100000000 | bytes 67108864 | tf_op jit(solution)/shard_map/fit_and_sum/pallas_call | solution.py:605
  150.1 0.8 copy.13
  150.9 0.6 copy.14
Async XLA Ops:
  1.7 19.6 %collective-permute-start.1 = (f32[16,4096]{1,0:T(8,128)S(1)}, f32[16,4096]{1,0:T(8,128)S(1)}, u32[]{:S(2)}, u32[]{:S(2)}) collective-permute-start(f32[16,4096]{1,0:T(8,128)S(1)} %get-tuple-element.12), channel_id=1, source_target_pairs={{1,0},{2,1},{3,2},{4,3},{5,4},{6,5},{7,6},{9,8},{10,9},{11,10},{12... | collective-permute-start | bytes 786440 | tf_op jit(solution)/shard_map/ppermute | solution.py:625
  3.0 18.3 %collective-permute-start = (f32[16,4096]{1,0:T(8,128)S(1)}, f32[16,4096]{1,0:T(8,128)S(1)}, u32[]{:S(2)}, u32[]{:S(2)}) collective-permute-start(f32[16,4096]{1,0:T(8,128)S(1)} %get-tuple-element.13), channel_id=1, source_target_pairs={{0,1},{1,2},{2,3},{3,4},{4,5},{5,6},{6,7},{8,9},{9,10},{10,11},{11... | collective-permute-start | bytes 786440 | tf_op jit(solution)/shard_map/ppermute | solution.py:624
  6.1 0.8 copy-start.2
  6.8 0.7 copy-start.4
  7.5 13.9 %copy-start.5 = (bf16[512,256]{1,0:T(8,128)(2,1)S(1)}, bf16[512,256]{1,0:T(8,128)(2,1)}, u32[]{:S(2)}) copy-start(bf16[512,256]{1,0:T(8,128)(2,1)} %constant.9.clone.cl_ref) | copy-start | bytes 786436
  7.5 13.9 %copy-start.6 = (bf16[512,256]{1,0:T(8,128)(2,1)S(1)}, bf16[512,256]{1,0:T(8,128)(2,1)}, u32[]{:S(2)}) copy-start(bf16[512,256]{1,0:T(8,128)(2,1)} %constant.8.clone.ch_ref) | copy-start | bytes 786436
  7.5 13.9 %copy-start.7 = (bf16[128,160]{1,0:T(8,128)(2,1)S(1)}, bf16[128,160]{1,0:T(8,128)(2,1)}, u32[]{:S(2)}) copy-start(bf16[128,160]{1,0:T(8,128)(2,1)} %constant.11.clone.rl_ref) | copy-start | bytes 122884
  7.5 13.9 %copy-start.8 = (bf16[128,160]{1,0:T(8,128)(2,1)S(1)}, bf16[128,160]{1,0:T(8,128)(2,1)}, u32[]{:S(2)}) copy-start(bf16[128,160]{1,0:T(8,128)(2,1)} %constant.10.clone.rh_ref) | copy-start | bytes 122884
  18.1 3.2 %copy-start = (f32[16,512,256]{2,1,0:T(8,128)}, f32[16,512,256]{2,1,0:T(8,128)S(1)}, u32[]{:S(2)}) copy-start(f32[16,512,256]{2,1,0:T(8,128)S(1)} %get-tuple-element.10) | copy-start | bytes 25165828
  21.3 26.6 %copy-start.3 = (s32[16,16]{1,0:T(8,128)S(1)}, s32[16,16]{1,0:T(8,128)}, u32[]{:S(2)}) copy-start(s32[16,16]{1,0:T(8,128)} %owner_ref.1) | copy-start | bytes 3076
  44.7 3.2 %copy-start.1 = (f32[16,512,256]{2,1,0:T(8,128)}, f32[16,512,256]{2,1,0:T(8,128)S(1)}, u32[]{:S(2)}) copy-start(f32[16,512,256]{2,1,0:T(8,128)S(1)} %get-tuple-element.11) | copy-start | bytes 25165828
where the time goes:
time: 152 us; the launch traced here: 151 us
  Pallas kernels  136 us (89%)
  local copies, waits for them, and re-layouts  10.3 us (7%)
  starting transfers between devices  4.34 us (3%)
    pallas_call x1, Pallas kernels, fit_and_sum(): pl.pallas_call(coadd_kernel, in_specs=[vmem, vmem, vmem, vmem, hbm, hbm],...  102 us
    pallas_call x1, Pallas kernels, smooth(): pl.pallas_call(smooth_kernel, grid=(16,), in_specs=[pl.BlockSpec(memory_s...  23.3 us
    pallas_call x1, Pallas kernels, weigh(): pl.pallas_call(weigh_kernel, grid=(ROWS // rows,), in_specs=[pl.BlockSpec...  10.6 us
    unnamed x20, local copies, waits for them, and re-layouts  9.27 us
    ppermute x1, starting transfers between devices, per_device(): up = lax.ppermute(image[0, ROWS - HALO:, :], 'sky', up_pairs)  3.05 us
  transfers between devices with their start and end apart: 2, of which 0 were waited for; matrix products, arithmetic and copies ran while one was open for 0% of the time, Pallas kernels for 7%

commit v1 on v0

v1 whole, which is shorter than its diff:
```python
import functools

import jax
import jax.numpy as jnp
import numpy as np
from jax import lax
from jax.experimental import pallas as pl
from jax.experimental.pallas import tpu as pltpu
from jax.sharding import PartitionSpec as P

F32 = jnp.float32
BF16 = jnp.bfloat16
HIGH = lax.Precision.HIGHEST
MESH = pl.DeviceIdType.MESH
BIN = 16
RADIUS = 10
NEXP = 16
ROWS = 512
COLS = 4096
SKY = 8
BROWS = 32
BCOLS = 256
FOOT_BINS = 192
HALO = 16
LAMBDA_REG = 0.25
PRIOR = 1.0


def iota(shape, dim):
    return lax.broadcasted_iota(jnp.int32, shape, dim)


def center(index, total):
    return (2.0 * index.astype(F32) + 1.0) / total - 1.0


def cheb(order, t):
    if order == 0:
        return jnp.ones_like(t)
    if order == 1:
        return t
    return 2.0 * t * t - 1.0


def split(value):
    high = value.astype(BF16)
    return high, (value - high.astype(F32)).astype(BF16)


def taps_matrix(offset):
    total = np.sum(np.exp(-(np.arange(-RADIUS, RADIUS + 1) ** 2) / 50.0))
    exact = np.where(np.abs(offset) <= RADIUS, np.exp(-(offset**2) / 50.0) / total, 0.0)
    high = exact.astype(BF16)
    return jnp.asarray(high), jnp.asarray((exact - high.astype(np.float64)).astype(BF16))


def add_into(dst, terms, blocks, rows):
    per = rows // 64

    def body(i, carry):
        b, r = i // per, pl.multiple_of((i % per) * 64, 64)
        total = terms[0](b, r)
        for term in terms[1:]:
            total = total + term(b, r)
        dst(b, r, total)
        return carry

    lax.fori_loop(0, blocks * per, body, 0)


class Scatter:
    def __init__(self, part, lead, row0, rows, place, bufs, sems, first_sem):
        self.part, self.lead, self.row0, self.half = part, lead, row0, rows // 2
        self.me, self.sky = place
        self.f1p, self.f1m, self.rp, self.rm, self.f2p, self.f2m, self.r2p, self.r2m = bufs
        self.send_sems, self.recv_sems = sems
        self.sem = first_sem
        self.copies = {}

    def device(self, axis, shift):
        x, z = self.me
        if axis == 0:
            x = lax.rem(x + shift + 4, 4)
        else:
            z = lax.rem(z + shift + 4, 4)
        return (4 * x + z, self.sky)

    def group(self, dist, r):
        g = lax.rem(self.me[self.lead] + dist, 4)
        rows = pl.ds(self.row0 + r, self.half)
        return self.part.at[g, :, rows, :] if self.lead == 0 else self.part.at[:, g, rows, :]

    def send(self, key, src, dst, axis, shift):
        n = self.sem
        self.sem += 1
        copy = pltpu.make_async_remote_copy(
            src_ref=src, dst_ref=dst, send_sem=self.send_sems.at[n], recv_sem=self.recv_sems.at[n],
            device_id=self.device(axis, shift), device_id_type=MESH,
        )
        copy.start()
        self.copies[key] = copy

    def start1(self):
        self.send("1p", self.group(2, 0), self.f1p, self.lead, 1)
        self.send("1m", self.group(2, self.half), self.f1m, self.lead, -1)

    def start2p(self):
        self.send("2p", self.group(1, self.half), self.rp.at[:, pl.ds(self.half, self.half), :], self.lead, 1)

    def start2m(self):
        self.send("2m", self.group(3, 0), self.rm.at[:, pl.ds(0, self.half), :], self.lead, -1)

    def load(self, dist, shift):
        g = lax.rem(self.me[self.lead] + dist, 4)

        def get(b, r):
            rows = pl.ds(self.row0 + shift + r, 64)
            return self.part[g, b, rows, :] if self.lead == 0 else self.part[b, g, rows, :]

        return get

    def start3(self):
        for key, buf, dist, shift, to in (("p", self.f1p, 1, 0, 1), ("m", self.f1m, 3, self.half, -1)):
            self.copies["1" + key].wait_recv()

            def put(b, r, v, buf=buf):
                buf[b, pl.ds(r, 64), :] = v

            add_into(put, [lambda b, r, buf=buf: buf[b, pl.ds(r, 64), :], self.load(dist, shift)], 4, self.half)
            land = self.rp if to == 1 else self.rm
            self.send("3" + key, buf, land.at[:, pl.ds(shift, self.half), :], self.lead, to)

    def finish1(self):
        for key in ("2p", "2m", "3p", "3m"):
            self.copies[key].wait_recv()

        def put(b, r, v):
            self.rp[b, pl.ds(r, 64), :] = v

        add_into(
            put,
            [lambda b, r: self.rp[b, pl.ds(r, 64), :], lambda b, r: self.rm[b, pl.ds(r, 64), :], self.load(0, 0)],
            4, 2 * self.half,
        )
        axis = 1 - self.lead
        at = lambda dist: lax.rem(self.me[axis] + dist, 4)
        top, low = pl.ds(0, self.half), pl.ds(self.half, self.half)
        self.send("4p", self.rp.at[at(2), top, :], self.f2p, axis, 1)
        self.send("4m", self.rp.at[at(2), low, :], self.f2m, axis, -1)
        self.send("5p", self.rp.at[at(1), low, :], self.r2p.at[low, :], axis, 1)
        self.send("5m", self.rp.at[at(3), top, :], self.r2m.at[top, :], axis, -1)

    def start6(self):
        axis = 1 - self.lead
        for key, buf, dist, shift, to in (("p", self.f2p, 1, 0, 1), ("m", self.f2m, 3, self.half, -1)):
            self.copies["4" + key].wait_recv()
            g = lax.rem(self.me[axis] + dist, 4)

            def put(b, r, v, buf=buf):
                buf[pl.ds(r, 64), :] = v

            add_into(
                put,
                [lambda b, r, buf=buf: buf[pl.ds(r, 64), :],
                 lambda b, r, g=g, shift=shift: self.rp[g, pl.ds(shift + r, 64), :]],
                1, self.half,
            )
            land = self.r2p if to == 1 else self.r2m
            self.send("6" + key, buf, land.at[pl.ds(shift, self.half), :], axis, to)

    def finish2(self):
        for key in ("5p", "5m", "6p", "6m"):
            self.copies[key].wait_recv()

    def total(self, r):
        g = self.me[1 - self.lead]
        return self.rp[g, pl.ds(r, 64), :] + self.r2p[pl.ds(r, 64), :] + self.r2m[pl.ds(r, 64), :]

    def drain(self):
        for copy in self.copies.values():
            copy.wait_send()


def invert(system):
    lane, row = iota((NEXP, 128), 1), iota((NEXP, 128), 0)
    work = jnp.concatenate([system, jnp.zeros((NEXP, 112), F32)], 1)
    work = work + jnp.where(lane == row + NEXP, 1.0, 0.0)
    for j in range(NEXP):
        pivot_row = work[j : j + 1, :] / work[j : j + 1, j : j + 1]
        factor = work[:, j : j + 1]
        work = jnp.where(row == j, pivot_row, work - factor * pivot_row)
    return work[:, NEXP : 2 * NEXP]


def moments(bins, me, band):
    image = jnp.concatenate([bins[:, 0, :], bins[:, 1, :]], 1)
    weight = jnp.concatenate([bins[:, 2, :], bins[:, 3, :]], 1)
    ws, ds = [], []
    for d in range(1, 9):
        other = pltpu.roll(weight, NEXP - d, 0)
        w = weight * other / (weight + other + 1.0)
        ws.append(w)
        ds.append(w * (image - pltpu.roll(image, NEXP - d, 0)))
    w, wd = jnp.concatenate(ws, 0), jnp.concatenate(ds, 0)

    def basis(rows, base):
        k, lane = iota((rows, 512), 0), iota((rows, 512), 1)
        y = center(BROWS * band + 2 * me + lane // 256, BCOLS)
        x = center(lane % 256, BCOLS)

        def pick(order, t):
            t2 = 2.0 * t * t - 1.0
            out = jnp.where(order == 0, 1.0, jnp.where(order == 1, t, t2))
            if base == 5:
                out = jnp.where(order == 3, 2.0 * t * t2 - t, out)
                out = jnp.where(order == 4, 2.0 * t2 * t2 - 1.0, out)
            return out

        return jnp.where(k < base * base, pick(k // base, y) * pick(k % base, x), 0.0)

    nt = (((1,), (1,)), ((), ()))
    gram = lax.dot_general(basis(32, 5), w, nt, precision=HIGH, preferred_element_type=F32)
    rhs = lax.dot_general(basis(16, 3), wd, nt, precision=HIGH, preferred_element_type=F32)
    return jnp.concatenate([gram, rhs], 0)


def solve_lanes(mom):
    m = lambda a, b: mom[5 * a + b : 5 * a + b + 1, :]
    cache = {}

    def entry(k, l):
        u, v, s, t = k // 3, k % 3, l // 3, l % 3
        key = tuple(sorted(((u + s, v + t), (abs(u - s), v + t), (u + s, abs(v - t)), (abs(u - s), abs(v - t)))))
        if key not in cache:
            cache[key] = 0.25 * ((m(*key[0]) + m(*key[1])) + (m(*key[2]) + m(*key[3])))
        return cache[key]

    a = [[entry(k, l) for l in range(k + 1)] for k in range(9)]
    b = [mom[32 + k : 33 + k, :] for k in range(9)]
    inv = [None] * 9
    for j in range(9):
        inv[j] = 1.0 / a[j][j]
        for k in range(j + 1, 9):
            f = a[k][j] * inv[j]
            for l in range(j + 1, k + 1):
                a[k][l] = a[k][l] - f * a[l][j]
            b[k] = b[k] - f * b[j]
    out = [None] * 9
    for j in reversed(range(9)):
        total = b[j]
        for k in range(j + 1, 9):
            total = total - a[k][j] * out[k]
        out[j] = total * inv[j]
    return out


SETS = (
    (4, lambda i: (2, i)),
    (3, lambda i: (lax.rem(i + 3, 4), 2)),
    (3, lambda i: (1, lax.rem(i + 3, 4))),
    (3, lambda i: (3, lax.rem(i + 3, 4))),
    (3, lambda i: (0, lax.rem(i + 3, 4))),
)
NUM_SCRATCH = 19


def coadd_kernel(image_hbm, variance_hbm, mask_hbm, foot_hbm, owner_hbm, ch_hbm, cl_hbm, rh_hbm, rl_hbm,
                 coadd_ref, offsets_ref, *scratch):
    (img, wv, sv, mask_ref, foot_ref, owner_ref, ch_ref, cl_ref, rh_ref, rl_ref, up_ref, down_ref, xh, xl, tx_ref,
     ty_ref, blocks, sums, bins_own), scratch = scratch[:NUM_SCRATCH], scratch[NUM_SCRATCH:]
    (bins, mom, sky_mom, exp_mom, offs, coefs), scratch = scratch[:6], scratch[6:]
    bufs, scratch = scratch[:48], scratch[48:]
    (small_sems, var_sems, img_sems, halo_s, halo_r, send_sems, recv_sems,
     bin_s, bin_r, sky_s, sky_r, exp_s, exp_r) = scratch
    me, band = lax.axis_index("exp"), lax.axis_index("sky")
    x, z = me // 4, lax.rem(me, 4)
    tall = ROWS + 2 * HALO

    barrier = pltpu.get_barrier_semaphore()
    for k in range(1, NEXP):
        pl.semaphore_signal(barrier, inc=1, device_id=(lax.rem(me + k, NEXP), band), device_id_type=MESH)
    for k in range(1, SKY):
        pl.semaphore_signal(barrier, inc=1, device_id=(me, lax.rem(band + k, SKY)), device_id_type=MESH)

    def place(rel):
        return lax.rem(x + rel[0], 4), lax.rem(z + rel[1], 4)

    def load_var(n, rel):
        cx, cz = place(rel)
        cols = pl.ds(pl.multiple_of(256 * (4 * cx + cz), 256), 256)
        return pltpu.make_async_copy(variance_hbm.at[0, :, cols], wv.at[cx, cz], var_sems.at[n])

    def load_img(n, rel):
        cx, cz = place(rel)
        cols = pl.ds(pl.multiple_of(256 * (4 * cx + cz), 256), 256)
        return pltpu.make_async_copy(image_hbm.at[0, :, cols], img.at[4 * cx + cz], img_sems.at[n])

    def each(fn, sets=range(5)):
        for s in sets:
            base = sum(SETS[t][0] for t in range(s))

            def body(i, carry, base=base, s=s):
                fn(base + i, SETS[s][1](i))
                return carry

            lax.fori_loop(0, SETS[s][0], body, 0)

    small = [
        pltpu.make_async_copy(src, dst, small_sems.at[n])
        for n, (src, dst) in enumerate((
            (mask_hbm.at[0], mask_ref), (foot_hbm, foot_ref), (owner_hbm, owner_ref),
            (ch_hbm, ch_ref), (cl_hbm, cl_ref), (rh_hbm, rh_ref), (rl_hbm, rl_ref),
        ))
    ]
    for copy in small[:2]:
        copy.start()
    each(lambda n, rel: load_var(n, rel).start())
    each(lambda n, rel: load_img(n, rel).start())
    for copy in small[2:]:
        copy.start()

    for copy in small[:2]:
        copy.wait()
    start = foot_ref[me]
    cell = iota((BROWS, BCOLS), 1)
    inside = (cell >= start) & (cell < start + FOOT_BINS)
    blocks[...] = jnp.where(inside, mask_ref[...].astype(F32), 0.0).astype(BF16)

    def onehot(m):
        hit = iota((256, 256), 0) == 16 * m + iota((256, 256), 1) // BIN
        return jnp.where(hit, 1.0, 0.0).astype(BF16)

    def weights(n, rel):
        load_var(n, rel).wait()
        cx, cz = place(rel)
        wide = jnp.dot(blocks[...], onehot(4 * cx + cz), preferred_element_type=F32)
        for r in range(4):
            rows = slice(128 * r, 128 * r + 128)
            keep = jnp.broadcast_to(wide[8 * r : 8 * r + 8][:, None, :], (8, BIN, 256)).reshape(128, 256)
            w = keep * (1.0 / wv[cx, cz, rows, :])
            wv[cx, cz, rows, :] = w
            sums[4 * cx + cz, 8 * r : 8 * r + 8, :] = jnp.sum(w.reshape(8, BIN, 256), axis=1)

    where = ((x, z), band)
    take = lambda n: bufs[8 * n : 8 * n + 8]
    sems = (send_sems, recv_sems)
    den = [Scatter(wv, h, 256 * h, 256, where, take(h), sems, 12 * h) for h in range(2)]
    num = [Scatter(sv, h, 256 * h + 128 * q, 128, where, take(2 + 2 * q + h), sems, 12 * (2 + 2 * q + h))
           for q in range(2) for h in range(2)]

    each(weights, [0])
    pl.semaphore_wait(barrier, NEXP + SKY - 2)
    den[0].start1()
    halos = []
    for n, (rows, dst, to) in enumerate(((ROWS - HALO, up_ref, band + 1), (0, down_ref, band + SKY - 1))):
        copy = pltpu.make_async_remote_copy(
            src_ref=image_hbm.at[0, pl.ds(rows, HALO), :], dst_ref=dst, send_sem=halo_s.at[n], recv_sem=halo_r.at[n],
            device_id=(me, lax.rem(to, SKY)), device_id_type=MESH,
        )
        copy.start()
        halos.append(copy)
    each(weights, [1])
    den[1].start1()
    each(weights, [2])
    den[0].start2p()
    each(weights, [3])
    den[0].start2m()
    each(weights, [4])
    den[1].start2p()
    den[1].start2m()

    def image_sums(n, rel):
        load_img(n, rel).wait()
        cx, cz = place(rel)
        m = 4 * cx + cz
        parts = []
        for r in range(4):
            parts.append(jnp.sum(img[m, 128 * r : 128 * r + 128, :].reshape(8, BIN, 256), axis=1))
        both = jnp.concatenate([jnp.concatenate(parts, 0) * (1.0 / (BIN * BIN)), sums[m]], 0)
        high = both.astype(BF16)
        rest = both - high.astype(F32)
        mid = rest.astype(BF16)
        low = (rest - mid.astype(F32)).astype(BF16)
        got = lax.dot_general(
            jnp.concatenate([high, mid, low], 0), onehot(m), (((1,), (1,)), ((), ())), preferred_element_type=F32
        )
        binned[...] = binned[...] + (got[:64] + got[64:128] + got[128:])

    binned = bins_own.at[NEXP]
    binned[...] = jnp.zeros((64, BCOLS), F32)
    each(image_sums)
    for m in range(NEXP):
        tile = [binned[2 * m : 2 * m + 2, :], binned[32 + 2 * m : 34 + 2 * m, :], jnp.zeros((4, BCOLS), F32)]
        bins_own[m, 0:8, :] = jnp.concatenate(tile, 0)
    bin_copies = []
    for k in range(1, NEXP):
        to = lax.rem(me + k, NEXP)
        copy = pltpu.make_async_remote_copy(
            src_ref=bins_own.at[to, pl.ds(0, 8), :], dst_ref=bins.at[me], send_sem=bin_s.at[k], recv_sem=bin_r.at[k],
            device_id=(to, band), device_id_type=MESH,
        )
        copy.start()
        bin_copies.append(copy)
    bins[me] = bins_own[me, 0:8, :]

    for copy in small[2:]:
        copy.wait()
    for copy in halos:
        copy.wait_recv()

    def put(j, first, lane0, value):
        rows, width = value.shape
        col = 256 * j - 128 + lane0 + iota((1, width), 1)
        keep = (col >= BIN * start) & (col < BIN * (start + FOOT_BINS))
        high, low = split(jnp.where(keep, value, 0.0))
        xh[first : first + rows, lane0 : lane0 + width] = high
        xl[first : first + rows, lane0 : lane0 + width] = low

    def row_pass(value, out):
        high, low = split(value)
        for i in range(ROWS // 128):
            zh, zl = high[128 * i : 128 * i + 160], low[128 * i : 128 * i + 160]
            out(
                128 * i,
                jnp.dot(rh_ref[...], zh, preferred_element_type=F32)
                + jnp.dot(rl_ref[...], zh, preferred_element_type=F32)
                + jnp.dot(rh_ref[...], zl, preferred_element_type=F32),
            )

    def smooth(n, rel):
        cx, cz = place(rel)
        j = 4 * cx + cz
        before, after = jnp.maximum(j - 1, 0), jnp.minimum(j + 1, 15)
        lo = pl.multiple_of(jnp.maximum(256 * j - 128, 0), 128)
        mid = pl.multiple_of(256 * j, 128)
        hi = pl.multiple_of(jnp.minimum(256 * j + 256, COLS - 128), 128)
        for first, ref, known in ((0, up_ref, band > 0), (HALO + ROWS, down_ref, band < SKY - 1)):
            put(j, first, 0, jnp.where(known, ref[:, pl.ds(lo, 128)], 0.0))
            put(j, first, 128, jnp.where(known, ref[:, pl.ds(mid, 256)], 0.0))
            put(j, first, 384, jnp.where(known, ref[:, pl.ds(hi, 128)], 0.0))
        put(j, HALO, 0, img[before, :, 128:256])
        put(j, HALO, 128, img[j])
        put(j, HALO, 384, img[after, :, 0:128])
        xcol = center(256 * j - 128 + iota((16, 512), 1), COLS)
        order = iota((16, 512), 0)
        put(j, tall, 0, jnp.where(order == 0, 1.0, jnp.where(order == 1, xcol, 2.0 * xcol * xcol - 1.0)))
        across = (
            jnp.dot(xh[...], ch_ref[...], preferred_element_type=F32)
            + jnp.dot(xl[...], ch_ref[...], preferred_element_type=F32)
            + jnp.dot(xh[...], cl_ref[...], preferred_element_type=F32)
        )
        tx_ref[j] = across[tall : tall + 8]

        def out(r, part):
            sv[cx, cz, r : r + 128, :] = part

        row_pass(across[:tall], out)

    each(smooth, [0])

    owner = owner_ref[...].astype(F32)
    both = owner + owner.T
    eye = iota((NEXP, NEXP), 0) == iota((NEXP, NEXP), 1)
    degree = jnp.sum(both, axis=1, keepdims=True) + LAMBDA_REG
    inverse = invert(jnp.where(eye, degree, 0.0) - both)
    lane, row = iota((NEXP, 128), 1), iota((NEXP, 128), 0)
    first = lax.rem(lane, NEXP)
    shift = lane // NEXP + 1
    second = lax.rem(first + shift, NEXP)
    at_first, at_second = row == first, row == second
    partner = jnp.dot(both, jnp.where(at_second, 1.0, 0.0), precision=HIGH, preferred_element_type=F32)
    used = jnp.sum(jnp.where(at_first, partner, 0.0), axis=0, keepdims=True)
    used = jnp.where((shift[:1] == 8) & (first[:1] >= 8), 0.0, used)
    sign = jnp.where(at_first, 1.0, 0.0) - jnp.where(at_second, 1.0, 0.0)

    for copy in bin_copies:
        copy.wait_recv()
    own = moments(bins, me, band)
    mom[0] = own
    sky_mom[band] = own
    sky_copies = []
    for k in range(1, SKY):
        copy = pltpu.make_async_remote_copy(
            src_ref=mom.at[0], dst_ref=sky_mom.at[band], send_sem=sky_s.at[k], recv_sem=sky_r.at[k],
            device_id=(me, lax.rem(band + k, SKY)), device_id_type=MESH,
        )
        copy.start()
        sky_copies.append(copy)
    ty_row = band * ROWS - HALO + iota((tall, 128), 0)
    y = center(ty_row, ROWS * SKY)
    known = (ty_row >= 0) & (ty_row < ROWS * SKY)
    for u in range(3):

        def out(r, part, u=u):
            ty_ref[u, r : r + 128, :] = part

        row_pass(jnp.where(known, cheb(u, y), 0.0), out)
    for copy in sky_copies:
        copy.wait_recv()
    total = sky_mom[0]
    for k in range(1, SKY):
        total = total + sky_mom[k]
    mom[1] = total
    exp_mom[me] = total
    exp_copies = []
    for k in range(1, NEXP):
        copy = pltpu.make_async_remote_copy(
            src_ref=mom.at[1], dst_ref=exp_mom.at[me], send_sem=exp_s.at[k], recv_sem=exp_r.at[k],
            device_id=(lax.rem(me + k, NEXP), band), device_id_type=MESH,
        )
        copy.start()
        exp_copies.append(copy)
    for part in den:
        part.start3()
    each(smooth, [1])
    for copy in exp_copies:
        copy.wait_recv()
    total = exp_mom[0]
    for k in range(1, NEXP):
        total = total + exp_mom[k]
    fits = jnp.concatenate(solve_lanes(total) + [jnp.zeros((7, 128), F32)], 0)
    fits = jnp.where(used > 0.0, fits, 0.0)
    nt = (((1,), (1,)), ((), ()))
    right = lax.dot_general(sign, fits, nt, precision=HIGH, preferred_element_type=F32)
    answer = jnp.dot(inverse, right, precision=HIGH, preferred_element_type=F32)
    offsets_ref[...] = answer[:, :9]
    offs[:, 0:NEXP] = answer
    coef = offs[pl.ds(me, 1), :]
    for k in range(9):
        coefs[k : k + 1, :] = jnp.broadcast_to(coef[:, k : k + 1], (1, 256))

    def numerator(half, dist):
        g = lax.rem((x, z)[half] + dist, 4)

        def chunk(b, carry):
            cx, cz = (g, b) if half == 0 else (b, g)
            tx = tx_ref[4 * cx + cz]
            lines = []
            for u in range(3):
                line = coefs[3 * u : 3 * u + 1, :] * tx[0:1]
                for v in range(1, 3):
                    line = line + coefs[3 * u + v : 3 * u + v + 1, :] * tx[v : v + 1]
                lines.append(line)
            for i in range(4):
                rows = slice(256 * half + 64 * i, 256 * half + 64 * i + 64)
                back = None
                for u in range(3):
                    ty = ty_ref[u, rows, :]
                    term = jnp.concatenate([ty, ty], 1) * lines[u]
                    back = term if back is None else back + term
                sv[cx, cz, rows, :] = wv[cx, cz, rows, :] * (sv[cx, cz, rows, :] - back)
            return carry

        lax.fori_loop(0, 4, chunk, 0)

    numerator(0, 2)
    num[0].start1()
    numerator(1, 2)
    num[1].start1()
    each(smooth, [2])
    numerator(0, 1)
    num[0].start2p()
    each(smooth, [3])
    numerator(0, 3)
    num[0].start2m()
    each(smooth, [4])
    numerator(1, 1)
    num[1].start2p()
    numerator(1, 3)
    num[1].start2m()
    for part in num[2:]:
        part.start1()
        part.start2p()
        part.start2m()
    for half in range(2):
        numerator(half, 0)
    for part in den:
        part.finish1()
    for part in num[:2]:
        part.start3()
    for part in den:
        part.start6()
    for part in num[2:]:
        part.start3()
    for part in num[:2]:
        part.finish1()
    for part in den:
        part.finish2()
    for part in num[:2]:
        part.start6()
    for part in num[2:]:
        part.finish1()
    for part in num[2:]:
        part.start6()

    def finish(n):
        part = num[n]
        part.finish2()
        h, q = n % 2, n // 2

        def body(i, carry):
            r = pl.multiple_of(i * 64, 64)
            value = part.total(r) / (PRIOR + den[h].total(128 * q + r))
            coadd_ref[pl.ds(256 * h + 128 * q + r, 64), :] = value
            return carry

        lax.fori_loop(0, 2, body, 0)

    for n in range(4):
        finish(n)
    for copy in halos + bin_copies + sky_copies + exp_copies:
        copy.wait_send()
    for part in den + num:
        part.drain()


def per_device(image, variance, mask, foot_start, pair_owner):
    k, n = np.arange(512)[:, None], np.arange(256)[None, :]
    ch, cl = taps_matrix(k - n - 128)
    k, n = np.arange(160)[None, :], np.arange(128)[:, None]
    rh, rl = taps_matrix(k - n - HALO)
    big = lambda *shape: pltpu.VMEM(shape, F32)
    half = lambda *shape: pltpu.VMEM(shape, BF16)
    pieces = lambda r: [big(4, r // 2, 256), big(4, r // 2, 256), big(4, r, 256), big(4, r, 256),
                        big(r // 2, 256), big(r // 2, 256), big(r, 256), big(r, 256)]
    dma = lambda n: pltpu.SemaphoreType.DMA((n,))
    vmem = pl.BlockSpec(memory_space=pltpu.VMEM)
    tall = ROWS + 2 * HALO
    held = [
        big(16, ROWS, 256), big(4, 4, ROWS, 256), big(4, 4, ROWS, 256),
        pltpu.VMEM((BROWS, BCOLS), jnp.int32), pltpu.SMEM((NEXP,), jnp.int32), pltpu.VMEM((NEXP, NEXP), jnp.int32),
        half(512, 256), half(512, 256), half(128, 160), half(128, 160), big(HALO, COLS), big(HALO, COLS),
        half(tall + 16, 512), half(tall + 16, 512), big(16, 8, 256), big(3, ROWS, 128), half(BROWS, BCOLS),
        big(16, BROWS, 256), big(NEXP + 1, 64, BCOLS),
    ]
    fit = [big(NEXP, 8, BCOLS), big(2, 48, 128), big(SKY, 48, 128), big(NEXP, 48, 128), big(NEXP, 128), big(16, 256)]
    sems = [dma(7), dma(16), dma(16), dma(2), dma(2), dma(72), dma(72), dma(NEXP), dma(NEXP), dma(SKY), dma(SKY),
            dma(NEXP), dma(NEXP)]
    return tuple(pl.pallas_call(
        coadd_kernel,
        in_specs=[pl.BlockSpec(memory_space=pl.ANY)] * 9,
        out_specs=[vmem, vmem],
        out_shape=[jax.ShapeDtypeStruct((ROWS, 256), F32), jax.ShapeDtypeStruct((NEXP, 9), F32)],
        scratch_shapes=held + fit + pieces(256) * 2 + pieces(128) * 4 + sems,
        compiler_params=pltpu.CompilerParams(collective_id=0, has_side_effects=True, vmem_limit_bytes=56 << 20),
        name="coadd",
    )(image, variance, mask, foot_start, pair_owner, ch, cl, rh, rl))


def solution(mesh):
    placed = (P("exp", "sky", None), P("exp", "sky", None), P("exp", "sky", None), P(), P())
    return jax.shard_map(
        per_device, mesh=mesh, in_specs=placed, out_specs=(P("sky", "exp"), P()), check_vma=False
    )
```

time: 152 us -> 118 us (0.78)
  Pallas kernels: 136 us -> 114 us
  local copies, waits for them, and re-layouts: 10.3 us -> 3.16 us
  starting transfers between devices: 4.34 us -> 0 us
    pallas_call x3 -> x1, Pallas kernels: 136 us -> 114 us  [per_device(): pl.pallas_call(coadd_kernel, in_specs=[pl.BlockSpec(memory_space=pl.ANY)]...]
    unnamed x20 -> x2, local copies, waits for them, and re-layouts: 9.27 us -> 3.16 us
    ppermute x2 -> x0, starting transfers between devices: 4.34 us -> none  [the longest x1 3.05 us: per_device(): up = lax.ppermute(image[0, ROWS - HALO:, :], 'sky', up_pairs)]
  transfers between devices with their start and end apart: 2 -> 0, of which waited for: 0 -> 0; matrix products, arithmetic and copies ran while one was open for 0% -> 0% of each run, Pallas kernels for 7% -> 0%
where the time goes in v1:
time: 118 us
  Pallas kernels  114 us (97%)
  local copies, waits for them, and re-layouts  3.16 us (3%)
    pallas_call x1, Pallas kernels, per_device(): pl.pallas_call(coadd_kernel, in_specs=[pl.BlockSpec(memory_space=pl.ANY)]...  114 us
    unnamed x2, local copies, waits for them, and re-layouts  3.16 us

profile of v1, /device:TPU:0, one launch (start us, length us, event | category | flops | bytes accessed | tf_op | source)
XLA Modules:
  0.0 118.0 jit_solution(6778525168718129474)
XLA Ops:
  0.6 114.2 %coadd.1 = (f32[512,256]{1,0:T(8,128)}, f32[16,9]{1,0:T(8,128)}) custom-call(f32[1,512,4096]{2,1,0:T(8,128)} %image_hbm.1, f32[1,512,4096]{2,1,0:T(8,128)} %variance_hbm.1, s32[1,32,256]{2,1,0:T(8,128)} %mask_hbm.1, s32[16]{0:T(128)} %foot_hbm.1, s32[16,16]{1,0:T(8,128)} %owner_hbm.1, bf16[512,256]{1,0:T(8,128)(2,1)} %constant.8.clone.ch_hbm, ...), custom_call_target="tpu_custom_call" | custom-call | tf_op jit(solution)/shard_map/coadd/pallas_call | solution.py:639
  114.8 1.9 %copy.13 = f32[512,256]{1,0:T(8,128)} copy(f32[512,256]{1,0:T(8,128)} %get-tuple-element.4) | data formatting | bytes 1048576
  116.7 1.3 %copy.14 = f32[16,9]{1,0:T(8,128)} copy(f32[16,9]{1,0:T(8,128)} %get-tuple-element.5) | data formatting | bytes 1152

commit v2 on v1

--- a/solution.py
+++ b/solution.py
@@ -76,6 +76,7 @@
         self.send_sems, self.recv_sems = sems
         self.sem = first_sem
         self.copies = {}
+        self.first = {"p": [], "m": []}
 
     def device(self, axis, shift):
         x, z = self.me
@@ -99,10 +100,17 @@
         )
         copy.start()
         self.copies[key] = copy
+        return copy
 
     def start1(self):
-        self.send("1p", self.group(2, 0), self.f1p, self.lead, 1)
-        self.send("1m", self.group(2, self.half), self.f1m, self.lead, -1)
+        self.first["p"].append(self.send("1p", self.group(2, 0), self.f1p, self.lead, 1))
+        self.first["m"].append(self.send("1m", self.group(2, self.half), self.f1m, self.lead, -1))
+
+    def start1_chunk(self, dist):
+        b = lax.rem(self.me[1 - self.lead] + dist, 4)
+        key = str(dist)
+        self.first["p"].append(self.send("1p" + key, self.group(2, 0).at[b], self.f1p.at[b], self.lead, 1))
+        self.first["m"].append(self.send("1m" + key, self.group(2, self.half).at[b], self.f1m.at[b], self.lead, -1))
 
     def start2p(self):
         self.send("2p", self.group(1, self.half), self.rp.at[:, pl.ds(self.half, self.half), :], self.lead, 1)
@@ -121,7 +129,8 @@
 
     def start3(self):
         for key, buf, dist, shift, to in (("p", self.f1p, 1, 0, 1), ("m", self.f1m, 3, self.half, -1)):
-            self.copies["1" + key].wait_recv()
+            for copy in self.first[key]:
+                copy.wait_recv()
 
             def put(b, r, v, buf=buf):
                 buf[b, pl.ds(r, 64), :] = v
@@ -193,8 +202,8 @@
 
 
 def moments(bins, me, band):
-    image = jnp.concatenate([bins[:, 0, :], bins[:, 1, :]], 1)
-    weight = jnp.concatenate([bins[:, 2, :], bins[:, 3, :]], 1)
+    image = jnp.concatenate([bins[:, 0, :], bins[:, 4, :], bins[:, 1, :], bins[:, 5, :]], 1)
+    weight = jnp.concatenate([bins[:, 2, :], bins[:, 6, :], bins[:, 3, :], bins[:, 7, :]], 1)
     ws, ds = [], []
     for d in range(1, 9):
         other = pltpu.roll(weight, NEXP - d, 0)
@@ -221,7 +230,7 @@
     nt = (((1,), (1,)), ((), ()))
     gram = lax.dot_general(basis(32, 5), w, nt, precision=HIGH, preferred_element_type=F32)
     rhs = lax.dot_general(basis(16, 3), wd, nt, precision=HIGH, preferred_element_type=F32)
-    return jnp.concatenate([gram, rhs], 0)
+    return jnp.concatenate([gram[:25], rhs[:9], jnp.zeros((6, 128), F32)], 0)
 
 
 def solve_lanes(mom):
@@ -236,7 +245,7 @@
         return cache[key]
 
     a = [[entry(k, l) for l in range(k + 1)] for k in range(9)]
-    b = [mom[32 + k : 33 + k, :] for k in range(9)]
+    b = [mom[25 + k : 26 + k, :] for k in range(9)]
     inv = [None] * 9
     for j in range(9):
         inv[j] = 1.0 / a[j][j]
@@ -254,20 +263,23 @@
     return out
 
 
-SETS = (
-    (4, lambda i: (2, i)),
-    (3, lambda i: (lax.rem(i + 3, 4), 2)),
-    (3, lambda i: (1, lax.rem(i + 3, 4))),
-    (3, lambda i: (3, lax.rem(i + 3, 4))),
-    (3, lambda i: (0, lax.rem(i + 3, 4))),
-)
-NUM_SCRATCH = 19
+def early(n):
+    other = lax.rem((n - 1) // 2 + 3, 4) - 2
+    odd = lax.rem(n - 1, 2)
+    return 2 + odd * other, 2 + (1 - odd) * other
+
+
+def late(n):
+    return lax.rem((n - 7) // 3 + 3, 4), lax.rem(lax.rem(n - 7, 3) + 3, 4)
+
+
+NUM_SCRATCH = 20
 
 
 def coadd_kernel(image_hbm, variance_hbm, mask_hbm, foot_hbm, owner_hbm, ch_hbm, cl_hbm, rh_hbm, rl_hbm,
                  coadd_ref, offsets_ref, *scratch):
     (img, wv, sv, mask_ref, foot_ref, owner_ref, ch_ref, cl_ref, rh_ref, rl_ref, up_ref, down_ref, xh, xl, tx_ref,
-     ty_ref, blocks, sums, bins_own), scratch = scratch[:NUM_SCRATCH], scratch[NUM_SCRATCH:]
+     ty_ref, blocks, sums, binned, bins_own), scratch = scratch[:NUM_SCRATCH], scratch[NUM_SCRATCH:]
     (bins, mom, sky_mom, exp_mom, offs, coefs), scratch = scratch[:6], scratch[6:]
     bufs, scratch = scratch[:48], scratch[48:]
     (small_sems, var_sems, img_sems, halo_s, halo_r, send_sems, recv_sems,
@@ -295,15 +307,18 @@
         cols = pl.ds(pl.multiple_of(256 * (4 * cx + cz), 256), 256)
         return pltpu.make_async_copy(image_hbm.at[0, :, cols], img.at[4 * cx + cz], img_sems.at[n])
 
-    def each(fn, sets=range(5)):
-        for s in sets:
-            base = sum(SETS[t][0] for t in range(s))
-
-            def body(i, carry, base=base, s=s):
-                fn(base + i, SETS[s][1](i))
-                return carry
-
-            lax.fori_loop(0, SETS[s][0], body, 0)
+    def each(fn, lo=0, hi=16):
+        if lo == 0:
+            fn(0, (2, 2))
+        for first, last, rel in ((1, 7, early), (7, 16, late)):
+            first, last = max(lo, first), min(hi, last)
+            if first < last:
+
+                def body(n, carry, rel=rel):
+                    fn(n, rel(n))
+                    return carry
+
+                lax.fori_loop(first, last, body, 0)
 
     small = [
         pltpu.make_async_copy(src, dst, small_sems.at[n])
@@ -344,13 +359,14 @@
     where = ((x, z), band)
     take = lambda n: bufs[8 * n : 8 * n + 8]
     sems = (send_sems, recv_sems)
-    den = [Scatter(wv, h, 256 * h, 256, where, take(h), sems, 12 * h) for h in range(2)]
-    num = [Scatter(sv, h, 256 * h + 128 * q, 128, where, take(2 + 2 * q + h), sems, 12 * (2 + 2 * q + h))
+    den = [Scatter(wv, h, 256 * h, 256, where, take(h), sems, 18 * h) for h in range(2)]
+    num = [Scatter(sv, h, 256 * h + 128 * q, 128, where, take(2 + 2 * q + h), sems, 36 + 12 * (2 * q + h))
            for q in range(2) for h in range(2)]
 
-    each(weights, [0])
+    weights(0, (2, 2))
     pl.semaphore_wait(barrier, NEXP + SKY - 2)
-    den[0].start1()
+    for part in den:
+        part.start1_chunk(2)
     halos = []
     for n, (rows, dst, to) in enumerate(((ROWS - HALO, up_ref, band + 1), (0, down_ref, band + SKY - 1))):
         copy = pltpu.make_async_remote_copy(
@@ -359,15 +375,13 @@
         )
         copy.start()
         halos.append(copy)
-    each(weights, [1])
-    den[1].start1()
-    each(weights, [2])
-    den[0].start2p()
-    each(weights, [3])
-    den[0].start2m()
-    each(weights, [4])
-    den[1].start2p()
-    den[1].start2m()
+    for t in range(3):
+        dist = (3 + t) % 4
+        weights(1 + 2 * t, (2, dist))
+        den[0].start1_chunk(dist)
+        weights(2 + 2 * t, (dist, 2))
+        den[1].start1_chunk(dist)
+    each(weights, 7, 16)
 
     def image_sums(n, rel):
         load_img(n, rel).wait()
@@ -386,22 +400,24 @@
         )
         binned[...] = binned[...] + (got[:64] + got[64:128] + got[128:])
 
-    binned = bins_own.at[NEXP]
     binned[...] = jnp.zeros((64, BCOLS), F32)
     each(image_sums)
     for m in range(NEXP):
-        tile = [binned[2 * m : 2 * m + 2, :], binned[32 + 2 * m : 34 + 2 * m, :], jnp.zeros((4, BCOLS), F32)]
-        bins_own[m, 0:8, :] = jnp.concatenate(tile, 0)
+        tile = jnp.concatenate([binned[2 * m : 2 * m + 2, :], binned[32 + 2 * m : 34 + 2 * m, :]], 0)
+        bins_own[m] = jnp.concatenate([tile[:, :128], tile[:, 128:]], 0)
     bin_copies = []
     for k in range(1, NEXP):
         to = lax.rem(me + k, NEXP)
         copy = pltpu.make_async_remote_copy(
-            src_ref=bins_own.at[to, pl.ds(0, 8), :], dst_ref=bins.at[me], send_sem=bin_s.at[k], recv_sem=bin_r.at[k],
+            src_ref=bins_own.at[to], dst_ref=bins.at[me], send_sem=bin_s.at[k], recv_sem=bin_r.at[k],
             device_id=(to, band), device_id_type=MESH,
         )
         copy.start()
         bin_copies.append(copy)
-    bins[me] = bins_own[me, 0:8, :]
+    bins[me] = bins_own[me]
+    for part in den:
+        part.start2p()
+        part.start2m()
 
     for copy in small[2:]:
         copy.wait()
@@ -456,8 +472,6 @@
 
         row_pass(across[:tall], out)
 
-    each(smooth, [0])
-
     owner = owner_ref[...].astype(F32)
     both = owner + owner.T
     eye = iota((NEXP, NEXP), 0) == iota((NEXP, NEXP), 1)
@@ -473,6 +487,7 @@
     used = jnp.where((shift[:1] == 8) & (first[:1] >= 8), 0.0, used)
     sign = jnp.where(at_first, 1.0, 0.0) - jnp.where(at_second, 1.0, 0.0)
 
+    each(smooth, 0, 2)
     for copy in bin_copies:
         copy.wait_recv()
     own = moments(bins, me, band)
@@ -495,6 +510,7 @@
             ty_ref[u, r : r + 128, :] = part
 
         row_pass(jnp.where(known, cheb(u, y), 0.0), out)
+    each(smooth, 2, 4)
     for copy in sky_copies:
         copy.wait_recv()
     total = sky_mom[0]
@@ -512,7 +528,7 @@
         exp_copies.append(copy)
     for part in den:
         part.start3()
-    each(smooth, [1])
+    each(smooth, 4, 8)
     for copy in exp_copies:
         copy.wait_recv()
     total = exp_mom[0]
@@ -553,35 +569,30 @@
 
         lax.fori_loop(0, 4, chunk, 0)
 
-    numerator(0, 2)
-    num[0].start1()
-    numerator(1, 2)
-    num[1].start1()
-    each(smooth, [2])
-    numerator(0, 1)
-    num[0].start2p()
-    each(smooth, [3])
-    numerator(0, 3)
-    num[0].start2m()
-    each(smooth, [4])
-    numerator(1, 1)
-    num[1].start2p()
-    numerator(1, 3)
-    num[1].start2m()
+    for half in range(2):
+        numerator(half, 2)
+        num[half].start1()
     for part in num[2:]:
         part.start1()
+    each(smooth, 8, 16)
+    for half in range(2):
+        numerator(half, 1)
+        num[half].start2p()
+        numerator(half, 3)
+        num[half].start2m()
+    for part in num[2:]:
         part.start2p()
         part.start2m()
-    for half in range(2):
-        numerator(half, 0)
     for part in den:
         part.finish1()
     for part in num[:2]:
         part.start3()
+    for half in range(2):
+        numerator(half, 0)
+    for part in num[2:]:
+        part.start3()
     for part in den:
         part.start6()
-    for part in num[2:]:
-        part.start3()
     for part in num[:2]:
         part.finish1()
     for part in den:
@@ -631,20 +642,21 @@
         pltpu.VMEM((BROWS, BCOLS), jnp.int32), pltpu.SMEM((NEXP,), jnp.int32), pltpu.VMEM((NEXP, NEXP), jnp.int32),
         half(512, 256), half(512, 256), half(128, 160), half(128, 160), big(HALO, COLS), big(HALO, COLS),
         half(tall + 16, 512), half(tall + 16, 512), big(16, 8, 256), big(3, ROWS, 128), half(BROWS, BCOLS),
-        big(16, BROWS, 256), big(NEXP + 1, 64, BCOLS),
+        big(16, BROWS, 256), big(64, BCOLS), big(NEXP, 8, 128),
     ]
-    fit = [big(NEXP, 8, BCOLS), big(2, 48, 128), big(SKY, 48, 128), big(NEXP, 48, 128), big(NEXP, 128), big(16, 256)]
-    sems = [dma(7), dma(16), dma(16), dma(2), dma(2), dma(72), dma(72), dma(NEXP), dma(NEXP), dma(SKY), dma(SKY),
+    fit = [big(NEXP, 8, 128), big(2, 40, 128), big(SKY, 40, 128), big(NEXP, 40, 128), big(NEXP, 128), big(16, 256)]
+    sems = [dma(7), dma(16), dma(16), dma(2), dma(2), dma(84), dma(84), dma(NEXP), dma(NEXP), dma(SKY), dma(SKY),
             dma(NEXP), dma(NEXP)]
     return tuple(pl.pallas_call(
         coadd_kernel,
-        in_specs=[pl.BlockSpec(memory_space=pl.ANY)] * 9,
+        in_specs=[pl.BlockSpec(memory_space=pltpu.HBM)] * 9,
         out_specs=[vmem, vmem],
         out_shape=[jax.ShapeDtypeStruct((ROWS, 256), F32), jax.ShapeDtypeStruct((NEXP, 9), F32)],
         scratch_shapes=held + fit + pieces(256) * 2 + pieces(128) * 4 + sems,
-        compiler_params=pltpu.CompilerParams(collective_id=0, has_side_effects=True, vmem_limit_bytes=56 << 20),
+        compiler_params=pltpu.CompilerParams(collective_id=0, has_side_effects=True, vmem_limit_bytes=48 << 20),
         name="coadd",
-    )(image, variance, mask, foot_start, pair_owner, ch, cl, rh, rl))
+    )(*(pltpu.with_memory_space_constraint(a, pltpu.HBM)
+        for a in (image, variance, mask, foot_start, pair_owner, ch, cl, rh, rl))))
 
 
 def solution(mesh):

time: 118 us -> 105 us (0.89)
  Pallas kernels: 114 us -> 103 us
  local copies, waits for them, and re-layouts: 3.16 us -> 1.39 us
    pallas_call x1, Pallas kernels: 114 us -> 103 us  [per_device(): pl.pallas_call(coadd_kernel, in_specs=[pl.BlockSpec(memory_space=pltpu.HB...]
    unnamed x2, local copies, waits for them, and re-layouts: 3.16 us -> 1.39 us
where the time goes in v2:
time: 105 us
  Pallas kernels  103 us (98%)
  local copies, waits for them, and re-layouts  1.39 us (1%)
    pallas_call x1, Pallas kernels, per_device(): pl.pallas_call(coadd_kernel, in_specs=[pl.BlockSpec(memory_space=pltpu.HB...  103 us

profile of v2, /device:TPU:0, one launch (start us, length us, event | category | flops | bytes accessed | tf_op | source)
XLA Modules:
  0.0 104.9 jit_solution(11882824358350304349)
XLA Ops:
  0.6 102.9 %coadd.1 = (f32[512,256]{1,0:T(8,128)S(1)}, f32[16,9]{1,0:T(8,128)S(1)}) custom-call(f32[1,512,4096]{2,1,0:T(8,128)} %image_hbm.1, f32[1,512,4096]{2,1,0:T(8,128)} %variance_hbm.1, s32[1,32,256]{2,1,0:T(8,128)} %mask_hbm.1, s32[16]{0:T(128)} %foot_hbm.1, s32[16,16]{1,0:T(8,128)} %owner_hbm.1, bf16[512,256]{1,0:T(8,128)(2,1)} %constant.8.clone.ch_hbm, ...), custom_call_target="tpu_custom_call" | custom-call | tf_op jit(solution)/shard_map/coadd/pallas_call | solution.py:650
  103.5 0.8 copy.13
  104.3 0.6 copy.14

commit v3 on v2

--- a/solution.py
+++ b/solution.py
@@ -23,6 +23,8 @@
 FOOT_BINS = 192
 HALO = 16
 LAMBDA_REG = 0.25
+DEN_ROWS = (240, 272)
+NUM_ROWS = (224, 288)
 PRIOR = 1.0
 
 
@@ -54,29 +56,17 @@
     return jnp.asarray(high), jnp.asarray((exact - high.astype(np.float64)).astype(BF16))
 
 
-def add_into(dst, terms, blocks, rows):
-    per = rows // 64
-
-    def body(i, carry):
-        b, r = i // per, pl.multiple_of((i % per) * 64, 64)
-        total = terms[0](b, r)
-        for term in terms[1:]:
-            total = total + term(b, r)
-        dst(b, r, total)
-        return carry
-
-    lax.fori_loop(0, blocks * per, body, 0)
-
-
 class Scatter:
-    def __init__(self, part, lead, row0, rows, place, bufs, sems, first_sem):
+    def __init__(self, part, lead, row0, rows, place, foot, bufs, sems, packed):
         self.part, self.lead, self.row0, self.half = part, lead, row0, rows // 2
-        self.me, self.sky = place
-        self.f1p, self.f1m, self.rp, self.rm, self.f2p, self.f2m, self.r2p, self.r2m = bufs
-        self.send_sems, self.recv_sems = sems
-        self.sem = first_sem
+        self.me, self.sky, self.foot = place[0], place[1], foot
+        (self.f1p, self.f1m, self.rp, self.rm, self.f2p, self.f2m, self.r2p, self.r2m), rest = bufs[:8], bufs[8:]
+        self.packs, self.lands = rest or (None, None)
+        self.send_sems, self.recv_sems, self.counter = sems
+        self.packed = packed
         self.copies = {}
         self.first = {"p": [], "m": []}
+        self.second = []
 
     def device(self, axis, shift):
         x, z = self.me
@@ -86,14 +76,23 @@
             z = lax.rem(z + shift + 4, 4)
         return (4 * x + z, self.sky)
 
-    def group(self, dist, r):
-        g = lax.rem(self.me[self.lead] + dist, 4)
+    def to(self, dist):
+        return lax.rem(self.me[self.lead] + dist, 4)
+
+    def group(self, dist, r, chunks=(0, 4)):
         rows = pl.ds(self.row0 + r, self.half)
-        return self.part.at[g, :, rows, :] if self.lead == 0 else self.part.at[:, g, rows, :]
+        some = pl.ds(*chunks)
+        g = self.to(dist)
+        return self.part.at[g, some, rows, :] if self.lead == 0 else self.part.at[some, g, rows, :]
+
+    def own(self, b, dist, r):
+        rows = pl.ds(self.row0 + r, self.half)
+        g = self.to(dist)
+        return self.part[g, b, rows, :] if self.lead == 0 else self.part[b, g, rows, :]
 
     def send(self, key, src, dst, axis, shift):
-        n = self.sem
-        self.sem += 1
+        n = self.counter[0]
+        self.counter[0] += 1
         copy = pltpu.make_async_remote_copy(
             src_ref=src, dst_ref=dst, send_sem=self.send_sems.at[n], recv_sem=self.recv_sems.at[n],
             device_id=self.device(axis, shift), device_id_type=MESH,
@@ -102,9 +101,23 @@
         self.copies[key] = copy
         return copy
 
+    def send_group(self, key, packed, slot, dist, r, land, to):
+        if not packed:
+            return [self.send(key, self.group(dist, r), land, self.lead, to)]
+        raw = self.send(key, self.group(dist, r, (1, 2)), land.at[pl.ds(1, 2)], self.lead, to)
+        self.packs[slot] = self.own(0, dist, r) + self.own(3, dist, r)
+        return [raw, self.send(key + "s", self.packs.at[slot], self.lands.at[slot], self.lead, to)]
+
+    def apart(self, slot, b):
+        sender = self.foot[self.device(1, -1 if slot in (0, 2) else 1)[0]]
+        g = self.to({0: 1, 1: 3, 2: 0, 3: 0}[slot])
+        low = 256 * g + iota((1, 256), 1) >= BIN * sender
+        return jnp.where(low if b == 0 else jnp.logical_not(low), self.lands[slot], 0.0)
+
     def start1(self):
-        self.first["p"].append(self.send("1p", self.group(2, 0), self.f1p, self.lead, 1))
-        self.first["m"].append(self.send("1m", self.group(2, self.half), self.f1m, self.lead, -1))
+        h = self.half
+        self.first["p"] += self.send_group("1p", self.packed[0], 0, 2, 0, self.f1p, 1)
+        self.first["m"] += self.send_group("1m", self.packed[0], 1, 2, h, self.f1m, -1)
 
     def start1_chunk(self, dist):
         b = lax.rem(self.me[1 - self.lead] + dist, 4)
@@ -112,48 +125,52 @@
         self.first["p"].append(self.send("1p" + key, self.group(2, 0).at[b], self.f1p.at[b], self.lead, 1))
         self.first["m"].append(self.send("1m" + key, self.group(2, self.half).at[b], self.f1m.at[b], self.lead, -1))
 
-    def start2p(self):
-        self.send("2p", self.group(1, self.half), self.rp.at[:, pl.ds(self.half, self.half), :], self.lead, 1)
-
-    def start2m(self):
-        self.send("2m", self.group(3, 0), self.rm.at[:, pl.ds(0, self.half), :], self.lead, -1)
-
-    def load(self, dist, shift):
-        g = lax.rem(self.me[self.lead] + dist, 4)
-
-        def get(b, r):
-            rows = pl.ds(self.row0 + shift + r, 64)
-            return self.part[g, b, rows, :] if self.lead == 0 else self.part[b, g, rows, :]
-
-        return get
+    def start2(self):
+        h = self.half
+        self.second += self.send_group("2p", self.packed[1], 2, 1, h, self.rp.at[:, pl.ds(h, h), :], 1)
+        self.second += self.send_group("2m", self.packed[1], 3, 3, 0, self.rm.at[:, pl.ds(0, h), :], -1)
 
     def start3(self):
-        for key, buf, dist, shift, to in (("p", self.f1p, 1, 0, 1), ("m", self.f1m, 3, self.half, -1)):
+        h = self.half
+        for key, buf, dist, shift, land, slot, to in (
+            ("p", self.f1p, 1, 0, self.rp, 0, 1), ("m", self.f1m, 3, h, self.rm, 1, -1)
+        ):
             for copy in self.first[key]:
                 copy.wait_recv()
 
-            def put(b, r, v, buf=buf):
-                buf[b, pl.ds(r, 64), :] = v
-
-            add_into(put, [lambda b, r, buf=buf: buf[b, pl.ds(r, 64), :], self.load(dist, shift)], 4, self.half)
-            land = self.rp if to == 1 else self.rm
-            self.send("3" + key, buf, land.at[:, pl.ds(shift, self.half), :], self.lead, to)
+            def body(b, carry, buf=buf, dist=dist, shift=shift):
+                buf[b] = buf[b] + self.own(b, dist, shift)
+                return carry
+
+            if self.packed[0]:
+                for b in (0, 3):
+                    buf[b] = self.apart(slot, b) + self.own(b, dist, shift)
+                lax.fori_loop(1, 3, body, 0)
+            else:
+                lax.fori_loop(0, 4, body, 0)
+            self.send("3" + key, buf, land.at[:, pl.ds(shift, h), :], self.lead, to)
 
     def finish1(self):
-        for key in ("2p", "2m", "3p", "3m"):
-            self.copies[key].wait_recv()
-
-        def put(b, r, v):
-            self.rp[b, pl.ds(r, 64), :] = v
-
-        add_into(
-            put,
-            [lambda b, r: self.rp[b, pl.ds(r, 64), :], lambda b, r: self.rm[b, pl.ds(r, 64), :], self.load(0, 0)],
-            4, 2 * self.half,
-        )
+        h = self.half
+        top, low = pl.ds(0, h), pl.ds(h, h)
+        for copy in self.second + [self.copies["3p"], self.copies["3m"]]:
+            copy.wait_recv()
+
+        def body(b, carry):
+            for shift in (0, h):
+                rows = pl.ds(shift, h)
+                self.rp[b, rows, :] = self.rp[b, rows, :] + self.rm[b, rows, :] + self.own(b, 0, shift)
+            return carry
+
+        if self.packed[1]:
+            for b in (0, 3):
+                self.rp[b, top, :] = self.rp[b, top, :] + self.apart(3, b) + self.own(b, 0, 0)
+                self.rp[b, low, :] = self.apart(2, b) + self.rm[b, low, :] + self.own(b, 0, h)
+            lax.fori_loop(1, 3, body, 0)
+        else:
+            lax.fori_loop(0, 4, body, 0)
         axis = 1 - self.lead
         at = lambda dist: lax.rem(self.me[axis] + dist, 4)
-        top, low = pl.ds(0, self.half), pl.ds(self.half, self.half)
         self.send("4p", self.rp.at[at(2), top, :], self.f2p, axis, 1)
         self.send("4m", self.rp.at[at(2), low, :], self.f2m, axis, -1)
         self.send("5p", self.rp.at[at(1), low, :], self.r2p.at[low, :], axis, 1)
@@ -161,29 +178,20 @@
 
     def start6(self):
         axis = 1 - self.lead
-        for key, buf, dist, shift, to in (("p", self.f2p, 1, 0, 1), ("m", self.f2m, 3, self.half, -1)):
+        for key, buf, dist, shift, land, to in (
+            ("p", self.f2p, 1, 0, self.r2p, 1), ("m", self.f2m, 3, self.half, self.r2m, -1)
+        ):
             self.copies["4" + key].wait_recv()
             g = lax.rem(self.me[axis] + dist, 4)
-
-            def put(b, r, v, buf=buf):
-                buf[pl.ds(r, 64), :] = v
-
-            add_into(
-                put,
-                [lambda b, r, buf=buf: buf[pl.ds(r, 64), :],
-                 lambda b, r, g=g, shift=shift: self.rp[g, pl.ds(shift + r, 64), :]],
-                1, self.half,
-            )
-            land = self.r2p if to == 1 else self.r2m
-            self.send("6" + key, buf, land.at[pl.ds(shift, self.half), :], axis, to)
+            rows = pl.ds(shift, self.half)
+            buf[...] = buf[...] + self.rp[g, rows, :]
+            self.send("6" + key, buf, land.at[rows, :], axis, to)
 
     def finish2(self):
         for key in ("5p", "5m", "6p", "6m"):
             self.copies[key].wait_recv()
-
-    def total(self, r):
         g = self.me[1 - self.lead]
-        return self.rp[g, pl.ds(r, 64), :] + self.r2p[pl.ds(r, 64), :] + self.r2m[pl.ds(r, 64), :]
+        return self.rp[g] + self.r2p[...] + self.r2m[...]
 
     def drain(self):
         for copy in self.copies.values():
@@ -280,8 +288,8 @@
                  coadd_ref, offsets_ref, *scratch):
     (img, wv, sv, mask_ref, foot_ref, owner_ref, ch_ref, cl_ref, rh_ref, rl_ref, up_ref, down_ref, xh, xl, tx_ref,
      ty_ref, blocks, sums, binned, bins_own), scratch = scratch[:NUM_SCRATCH], scratch[NUM_SCRATCH:]
-    (bins, mom, sky_mom, exp_mom, offs, coefs), scratch = scratch[:6], scratch[6:]
-    bufs, scratch = scratch[:48], scratch[48:]
+    (bins, mom, sky_mom, exp_mom, offs, coefs, total_den), scratch = scratch[:7], scratch[7:]
+    bufs, scratch = scratch[:54], scratch[54:]
     (small_sems, var_sems, img_sems, halo_s, halo_r, send_sems, recv_sems,
      bin_s, bin_r, sky_s, sky_r, exp_s, exp_r) = scratch
     me, band = lax.axis_index("exp"), lax.axis_index("sky")
@@ -357,11 +365,14 @@
             sums[4 * cx + cz, 8 * r : 8 * r + 8, :] = jnp.sum(w.reshape(8, BIN, 256), axis=1)
 
     where = ((x, z), band)
-    take = lambda n: bufs[8 * n : 8 * n + 8]
-    sems = (send_sems, recv_sems)
-    den = [Scatter(wv, h, 256 * h, 256, where, take(h), sems, 18 * h) for h in range(2)]
-    num = [Scatter(sv, h, 256 * h + 128 * q, 128, where, take(2 + 2 * q + h), sems, 36 + 12 * (2 * q + h))
-           for q in range(2) for h in range(2)]
+    take = lambda n: bufs[18 * (n // 2) : 18 * (n // 2) + 8] if n % 2 == 0 else bufs[18 * (n // 2) + 8 : 18 * (n // 2) + 18]
+    sems = (send_sems, recv_sems, [0])
+    den = [Scatter(wv, h, DEN_ROWS[0] * h, DEN_ROWS[h], where, foot_ref, take(h), sems, (False, h == 1)) for h in range(2)]
+    num = [
+        Scatter(sv, h, NUM_ROWS[0] * h + NUM_ROWS[h] // 2 * q, NUM_ROWS[h] // 2, where, foot_ref, take(2 + 2 * q + h),
+                sems, (h == 1, h == 1))
+        for q in range(2) for h in range(2)
+    ]
 
     weights(0, (2, 2))
     pl.semaphore_wait(barrier, NEXP + SKY - 2)
@@ -416,8 +427,7 @@
         bin_copies.append(copy)
     bins[me] = bins_own[me]
     for part in den:
-        part.start2p()
-        part.start2m()
+        part.start2()
 
     for copy in small[2:]:
         copy.wait()
@@ -557,8 +567,9 @@
                 for v in range(1, 3):
                     line = line + coefs[3 * u + v : 3 * u + v + 1, :] * tx[v : v + 1]
                 lines.append(line)
+            step = NUM_ROWS[half] // 4
             for i in range(4):
-                rows = slice(256 * half + 64 * i, 256 * half + 64 * i + 64)
+                rows = slice(NUM_ROWS[0] * half + step * i, NUM_ROWS[0] * half + step * i + step)
                 back = None
                 for u in range(3):
                     ty = ty_ref[u, rows, :]
@@ -577,12 +588,10 @@
     each(smooth, 8, 16)
     for half in range(2):
         numerator(half, 1)
-        num[half].start2p()
         numerator(half, 3)
-        num[half].start2m()
+        num[half].start2()
     for part in num[2:]:
-        part.start2p()
-        part.start2m()
+        part.start2()
     for part in den:
         part.finish1()
     for part in num[:2]:
@@ -595,8 +604,8 @@
         part.start6()
     for part in num[:2]:
         part.finish1()
-    for part in den:
-        part.finish2()
+    for h in range(2):
+        total_den[DEN_ROWS[0] * h : DEN_ROWS[0] * h + DEN_ROWS[h], :] = PRIOR + den[h].finish2()
     for part in num[:2]:
         part.start6()
     for part in num[2:]:
@@ -604,21 +613,9 @@
     for part in num[2:]:
         part.start6()
 
-    def finish(n):
-        part = num[n]
-        part.finish2()
-        h, q = n % 2, n // 2
-
-        def body(i, carry):
-            r = pl.multiple_of(i * 64, 64)
-            value = part.total(r) / (PRIOR + den[h].total(128 * q + r))
-            coadd_ref[pl.ds(256 * h + 128 * q + r, 64), :] = value
-            return carry
-
-        lax.fori_loop(0, 2, body, 0)
-
-    for n in range(4):
-        finish(n)
+    for part in num:
+        rows = slice(part.row0, part.row0 + 2 * part.half)
+        coadd_ref[rows, :] = part.finish2() / total_den[rows, :]
     for copy in halos + bin_copies + sky_copies + exp_copies:
         copy.wait_send()
     for part in den + num:
@@ -632,8 +629,9 @@
     rh, rl = taps_matrix(k - n - HALO)
     big = lambda *shape: pltpu.VMEM(shape, F32)
     half = lambda *shape: pltpu.VMEM(shape, BF16)
-    pieces = lambda r: [big(4, r // 2, 256), big(4, r // 2, 256), big(4, r, 256), big(4, r, 256),
-                        big(r // 2, 256), big(r // 2, 256), big(r, 256), big(r, 256)]
+    piece = lambda r: [big(4, r // 2, 256), big(4, r // 2, 256), big(4, r, 256), big(4, r, 256),
+                       big(r // 2, 256), big(r // 2, 256), big(r, 256), big(r, 256)]
+    pieces = lambda a, b: piece(a) + piece(b) + [big(4, b // 2, 256), big(4, b // 2, 256)]
     dma = lambda n: pltpu.SemaphoreType.DMA((n,))
     vmem = pl.BlockSpec(memory_space=pltpu.VMEM)
     tall = ROWS + 2 * HALO
@@ -644,16 +642,17 @@
         half(tall + 16, 512), half(tall + 16, 512), big(16, 8, 256), big(3, ROWS, 128), half(BROWS, BCOLS),
         big(16, BROWS, 256), big(64, BCOLS), big(NEXP, 8, 128),
     ]
-    fit = [big(NEXP, 8, 128), big(2, 40, 128), big(SKY, 40, 128), big(NEXP, 40, 128), big(NEXP, 128), big(16, 256)]
-    sems = [dma(7), dma(16), dma(16), dma(2), dma(2), dma(84), dma(84), dma(NEXP), dma(NEXP), dma(SKY), dma(SKY),
+    fit = [big(NEXP, 8, 128), big(2, 40, 128), big(SKY, 40, 128), big(NEXP, 40, 128), big(NEXP, 128), big(16, 256),
+           big(ROWS, 256)]
+    sems = [dma(7), dma(16), dma(16), dma(2), dma(2), dma(96), dma(96), dma(NEXP), dma(NEXP), dma(SKY), dma(SKY),
             dma(NEXP), dma(NEXP)]
     return tuple(pl.pallas_call(
         coadd_kernel,
         in_specs=[pl.BlockSpec(memory_space=pltpu.HBM)] * 9,
         out_specs=[vmem, vmem],
         out_shape=[jax.ShapeDtypeStruct((ROWS, 256), F32), jax.ShapeDtypeStruct((NEXP, 9), F32)],
-        scratch_shapes=held + fit + pieces(256) * 2 + pieces(128) * 4 + sems,
-        compiler_params=pltpu.CompilerParams(collective_id=0, has_side_effects=True, vmem_limit_bytes=48 << 20),
+        scratch_shapes=held + fit + pieces(*DEN_ROWS) + pieces(NUM_ROWS[0] // 2, NUM_ROWS[1] // 2) * 2 + sems,
+        compiler_params=pltpu.CompilerParams(collective_id=0, has_side_effects=True, vmem_limit_bytes=52 << 20),
         name="coadd",
     )(*(pltpu.with_memory_space_constraint(a, pltpu.HBM)
         for a in (image, variance, mask, foot_start, pair_owner, ch, cl, rh, rl))))

time: 105 us -> 102 us (0.971)
  Pallas kernels: 103 us -> 100 us
    pallas_call x1, Pallas kernels: 103 us -> 100 us  [per_device(): pl.pallas_call(coadd_kernel, in_specs=[pl.BlockSpec(memory_space=pltpu.HB...]
where the time goes in v3:
time: 102 us
  Pallas kernels  100 us (98%)
  local copies, waits for them, and re-layouts  1.39 us (1%)
    pallas_call x1, Pallas kernels, per_device(): pl.pallas_call(coadd_kernel, in_specs=[pl.BlockSpec(memory_space=pltpu.HB...  100 us

profile of v3, /device:TPU:0, one launch (start us, length us, event | category | flops | bytes accessed | tf_op | source)
XLA Modules:
  0.0 102.2 jit_solution(5968781295484388378)
XLA Ops:
  0.6 100.2 %coadd.1 = (f32[512,256]{1,0:T(8,128)S(1)}, f32[16,9]{1,0:T(8,128)S(1)}) custom-call(f32[1,512,4096]{2,1,0:T(8,128)} %image_hbm.1, f32[1,512,4096]{2,1,0:T(8,128)} %variance_hbm.1, s32[1,32,256]{2,1,0:T(8,128)} %mask_hbm.1, s32[16]{0:T(128)} %foot_hbm.1, s32[16,16]{1,0:T(8,128)} %owner_hbm.1, bf16[512,256]{1,0:T(8,128)(2,1)} %constant.8.clone.ch_hbm, ...), custom_call_target="tpu_custom_call" | custom-call | tf_op jit(solution)/shard_map/coadd/pallas_call | solution.py:649
  100.8 0.8 copy.13
  101.6 0.6 copy.14

commit v4 on v3

--- a/solution.py
+++ b/solution.py
@@ -67,6 +67,7 @@
         self.copies = {}
         self.first = {"p": [], "m": []}
         self.second = []
+        self.third = []
 
     def device(self, axis, shift):
         x, z = self.me
@@ -130,13 +131,14 @@
         self.second += self.send_group("2p", self.packed[1], 2, 1, h, self.rp.at[:, pl.ds(h, h), :], 1)
         self.second += self.send_group("2m", self.packed[1], 3, 3, 0, self.rm.at[:, pl.ds(0, h), :], -1)
 
-    def start3(self):
+    def start3(self, lo=0, hi=4):
         h = self.half
         for key, buf, dist, shift, land, slot, to in (
             ("p", self.f1p, 1, 0, self.rp, 0, 1), ("m", self.f1m, 3, h, self.rm, 1, -1)
         ):
-            for copy in self.first[key]:
-                copy.wait_recv()
+            if lo == 0:
+                for copy in self.first[key]:
+                    copy.wait_recv()
 
             def body(b, carry, buf=buf, dist=dist, shift=shift):
                 buf[b] = buf[b] + self.own(b, dist, shift)
@@ -144,16 +146,20 @@
 
             if self.packed[0]:
                 for b in (0, 3):
-                    buf[b] = self.apart(slot, b) + self.own(b, dist, shift)
-                lax.fori_loop(1, 3, body, 0)
+                    if lo <= b < hi:
+                        buf[b] = self.apart(slot, b) + self.own(b, dist, shift)
+                lax.fori_loop(max(lo, 1), min(hi, 3), body, 0)
             else:
-                lax.fori_loop(0, 4, body, 0)
-            self.send("3" + key, buf, land.at[:, pl.ds(shift, h), :], self.lead, to)
+                lax.fori_loop(lo, hi, body, 0)
+            some = pl.ds(lo, hi - lo)
+            self.third.append(
+                self.send("3" + key + str(lo), buf.at[some], land.at[some, pl.ds(shift, h), :], self.lead, to)
+            )
 
     def finish1(self):
         h = self.half
         top, low = pl.ds(0, h), pl.ds(h, h)
-        for copy in self.second + [self.copies["3p"], self.copies["3m"]]:
+        for copy in self.second + self.third:
             copy.wait_recv()
 
         def body(b, carry):
@@ -288,10 +294,10 @@
                  coadd_ref, offsets_ref, *scratch):
     (img, wv, sv, mask_ref, foot_ref, owner_ref, ch_ref, cl_ref, rh_ref, rl_ref, up_ref, down_ref, xh, xl, tx_ref,
      ty_ref, blocks, sums, binned, bins_own), scratch = scratch[:NUM_SCRATCH], scratch[NUM_SCRATCH:]
-    (bins, mom, sky_mom, exp_mom, offs, coefs, total_den), scratch = scratch[:7], scratch[7:]
+    (bins, mom, sky_mom, axis_mom, offs, coefs, total_den), scratch = scratch[:7], scratch[7:]
     bufs, scratch = scratch[:54], scratch[54:]
     (small_sems, var_sems, img_sems, halo_s, halo_r, send_sems, recv_sems,
-     bin_s, bin_r, sky_s, sky_r, exp_s, exp_r) = scratch
+     bin_s, bin_r, sky_s, sky_r, axis_s, axis_r) = scratch
     me, band = lax.axis_index("exp"), lax.axis_index("sky")
     x, z = me // 4, lax.rem(me, 4)
     tall = ROWS + 2 * HALO
@@ -526,24 +532,32 @@
     total = sky_mom[0]
     for k in range(1, SKY):
         total = total + sky_mom[k]
-    mom[1] = total
-    exp_mom[me] = total
-    exp_copies = []
-    for k in range(1, NEXP):
-        copy = pltpu.make_async_remote_copy(
-            src_ref=mom.at[1], dst_ref=exp_mom.at[me], send_sem=exp_s.at[k], recv_sem=exp_r.at[k],
-            device_id=(lax.rem(me + k, NEXP), band), device_id_type=MESH,
-        )
-        copy.start()
-        exp_copies.append(copy)
-    for part in den:
-        part.start3()
-    each(smooth, 4, 8)
-    for copy in exp_copies:
-        copy.wait_recv()
-    total = exp_mom[0]
-    for k in range(1, NEXP):
-        total = total + exp_mom[k]
+    def exchange(n, total, at, device):
+        mom[1 + n] = total
+        axis_mom[n, at] = total
+        copies = []
+        for k in range(1, 4):
+            copy = pltpu.make_async_remote_copy(
+                src_ref=mom.at[1 + n], dst_ref=axis_mom.at[n, at], send_sem=axis_s.at[n, k], recv_sem=axis_r.at[n, k],
+                device_id=(device(k), band), device_id_type=MESH,
+            )
+            copy.start()
+            copies.append(copy)
+        return copies
+
+    def gathered(n, copies):
+        for copy in copies:
+            copy.wait_recv()
+        return (axis_mom[n, 0] + axis_mom[n, 1]) + (axis_mom[n, 2] + axis_mom[n, 3])
+
+    x_copies = exchange(0, total, x, lambda k: 4 * lax.rem(x + k, 4) + z)
+    den[0].start3()
+    den[1].start3(0, 2)
+    each(smooth, 4, 5)
+    z_copies = exchange(1, gathered(0, x_copies), z, lambda k: 4 * x + lax.rem(z + k, 4))
+    den[1].start3(2, 4)
+    each(smooth, 5, 8)
+    total = gathered(1, z_copies)
     fits = jnp.concatenate(solve_lanes(total) + [jnp.zeros((7, 128), F32)], 0)
     fits = jnp.where(used > 0.0, fits, 0.0)
     nt = (((1,), (1,)), ((), ()))
@@ -616,7 +630,7 @@
     for part in num:
         rows = slice(part.row0, part.row0 + 2 * part.half)
         coadd_ref[rows, :] = part.finish2() / total_den[rows, :]
-    for copy in halos + bin_copies + sky_copies + exp_copies:
+    for copy in halos + bin_copies + sky_copies + x_copies + z_copies:
         copy.wait_send()
     for part in den + num:
         part.drain()
@@ -642,10 +656,10 @@
         half(tall + 16, 512), half(tall + 16, 512), big(16, 8, 256), big(3, ROWS, 128), half(BROWS, BCOLS),
         big(16, BROWS, 256), big(64, BCOLS), big(NEXP, 8, 128),
     ]
-    fit = [big(NEXP, 8, 128), big(2, 40, 128), big(SKY, 40, 128), big(NEXP, 40, 128), big(NEXP, 128), big(16, 256),
+    fit = [big(NEXP, 8, 128), big(3, 40, 128), big(SKY, 40, 128), big(2, 4, 40, 128), big(NEXP, 128), big(16, 256),
            big(ROWS, 256)]
-    sems = [dma(7), dma(16), dma(16), dma(2), dma(2), dma(96), dma(96), dma(NEXP), dma(NEXP), dma(SKY), dma(SKY),
-            dma(NEXP), dma(NEXP)]
+    sems = [dma(7), dma(16), dma(16), dma(2), dma(2), dma(104), dma(104), dma(NEXP), dma(NEXP), dma(SKY), dma(SKY),
+            pltpu.SemaphoreType.DMA((2, 4)), pltpu.SemaphoreType.DMA((2, 4))]
     return tuple(pl.pallas_call(
         coadd_kernel,
         in_specs=[pl.BlockSpec(memory_space=pltpu.HBM)] * 9,

time: 102 us -> 99.7 us (0.977)
  Pallas kernels: 100 us -> 97.6 us
    pallas_call x1, Pallas kernels: 100 us -> 97.6 us  [per_device(): pl.pallas_call(coadd_kernel, in_specs=[pl.BlockSpec(memory_space=pltpu.HB...]
where the time goes in v4:
time: 99.7 us; the launch traced here: 99.6 us
  Pallas kernels  97.6 us (98%)
  local copies, waits for them, and re-layouts  1.39 us (1%)
    pallas_call x1, Pallas kernels, per_device(): pl.pallas_call(coadd_kernel, in_specs=[pl.BlockSpec(memory_space=pltpu.HB...  97.6 us

profile of v4, /device:TPU:0, one launch (start us, length us, event | category | flops | bytes accessed | tf_op | source)
XLA Modules:
  0.0 99.6 jit_solution(1472258290162434141)
XLA Ops:
  0.6 97.6 %coadd.1 = (f32[512,256]{1,0:T(8,128)S(1)}, f32[16,9]{1,0:T(8,128)S(1)}) custom-call(f32[1,512,4096]{2,1,0:T(8,128)} %image_hbm.1, f32[1,512,4096]{2,1,0:T(8,128)} %variance_hbm.1, s32[1,32,256]{2,1,0:T(8,128)} %mask_hbm.1, s32[16]{0:T(128)} %foot_hbm.1, s32[16,16]{1,0:T(8,128)} %owner_hbm.1, bf16[512,256]{1,0:T(8,128)(2,1)} %constant.8.clone.ch_hbm, ...), custom_call_target="tpu_custom_call" | custom-call | tf_op jit(solution)/shard_map/coadd/pallas_call | solution.py:663
  98.2 0.8 copy.13
  99.0 0.6 copy.14

commit v5 on v4

--- a/solution.py
+++ b/solution.py
@@ -23,8 +23,9 @@
 FOOT_BINS = 192
 HALO = 16
 LAMBDA_REG = 0.25
-DEN_ROWS = (240, 272)
+DEN_ROWS = (224, 288)
 NUM_ROWS = (224, 288)
+NUM_PIECES = ((160, 208), (64, 80))
 PRIOR = 1.0
 
 
@@ -91,13 +92,20 @@
         g = self.to(dist)
         return self.part[g, b, rows, :] if self.lead == 0 else self.part[b, g, rows, :]
 
-    def send(self, key, src, dst, axis, shift):
+    def remote(self, src, dst, axis, shift):
         n = self.counter[0]
         self.counter[0] += 1
-        copy = pltpu.make_async_remote_copy(
+        return pltpu.make_async_remote_copy(
             src_ref=src, dst_ref=dst, send_sem=self.send_sems.at[n], recv_sem=self.recv_sems.at[n],
             device_id=self.device(axis, shift), device_id_type=MESH,
         )
+
+    def keep(self, key, copies, copy):
+        self.copies[key] = copy
+        copies.append(copy)
+
+    def send(self, key, src, dst, axis, shift):
+        copy = self.remote(src, dst, axis, shift)
         copy.start()
         self.copies[key] = copy
         return copy
@@ -122,9 +130,27 @@
 
     def start1_chunk(self, dist):
         b = lax.rem(self.me[1 - self.lead] + dist, 4)
-        key = str(dist)
-        self.first["p"].append(self.send("1p" + key, self.group(2, 0).at[b], self.f1p.at[b], self.lead, 1))
-        self.first["m"].append(self.send("1m" + key, self.group(2, self.half).at[b], self.f1m.at[b], self.lead, -1))
+        for key, r, buf, to in (("p", 0, self.f1p, 1), ("m", self.half, self.f1m, -1)):
+            if not self.packed[0]:
+                copy = self.remote(self.group(2, r).at[b], buf.at[b], self.lead, to)
+                copy.start()
+                self.keep("1" + key + str(dist), self.first[key], copy)
+                continue
+            for c in (1, 2):
+                name = "1" + key + str(c)
+                if name not in self.copies:
+                    self.keep(name, self.first[key], self.remote(self.group(2, r).at[c], buf.at[c], self.lead, to))
+
+                @pl.when(b == c)
+                def _(name=name):
+                    self.copies[name].start()
+
+    def start1_sum(self):
+        for key, slot, r, to in (("p", 0, 0, 1), ("m", 1, self.half, -1)):
+            self.packs[slot] = self.own(0, 2, r) + self.own(3, 2, r)
+            copy = self.remote(self.packs.at[slot], self.lands.at[slot], self.lead, to)
+            copy.start()
+            self.keep("1s" + key, self.first[key], copy)
 
     def start2(self):
         h = self.half
@@ -278,7 +304,8 @@
 
 
 def early(n):
-    other = lax.rem((n - 1) // 2 + 3, 4) - 2
+    t = (n - 1) // 2
+    other = t + t // 2 - 2
     odd = lax.rem(n - 1, 2)
     return 2 + odd * other, 2 + (1 - odd) * other
 
@@ -373,9 +400,9 @@
     where = ((x, z), band)
     take = lambda n: bufs[18 * (n // 2) : 18 * (n // 2) + 8] if n % 2 == 0 else bufs[18 * (n // 2) + 8 : 18 * (n // 2) + 18]
     sems = (send_sems, recv_sems, [0])
-    den = [Scatter(wv, h, DEN_ROWS[0] * h, DEN_ROWS[h], where, foot_ref, take(h), sems, (False, h == 1)) for h in range(2)]
+    den = [Scatter(wv, h, DEN_ROWS[0] * h, DEN_ROWS[h], where, foot_ref, take(h), sems, (h == 1, h == 1)) for h in range(2)]
     num = [
-        Scatter(sv, h, NUM_ROWS[0] * h + NUM_ROWS[h] // 2 * q, NUM_ROWS[h] // 2, where, foot_ref, take(2 + 2 * q + h),
+        Scatter(sv, h, NUM_ROWS[0] * h + NUM_PIECES[0][h] * q, NUM_PIECES[q][h], where, foot_ref, take(2 + 2 * q + h),
                 sems, (h == 1, h == 1))
         for q in range(2) for h in range(2)
     ]
@@ -393,11 +420,12 @@
         copy.start()
         halos.append(copy)
     for t in range(3):
-        dist = (3 + t) % 4
+        dist = (0, 1, 3)[t]
         weights(1 + 2 * t, (2, dist))
         den[0].start1_chunk(dist)
         weights(2 + 2 * t, (dist, 2))
         den[1].start1_chunk(dist)
+    den[1].start1_sum()
     each(weights, 7, 16)
 
     def image_sums(n, rel):
@@ -612,21 +640,20 @@
         part.start3()
     for half in range(2):
         numerator(half, 0)
+    for part in den:
+        part.start6()
     for part in num[2:]:
         part.start3()
-    for part in den:
-        part.start6()
     for part in num[:2]:
         part.finish1()
-    for h in range(2):
-        total_den[DEN_ROWS[0] * h : DEN_ROWS[0] * h + DEN_ROWS[h], :] = PRIOR + den[h].finish2()
+    for part in num[2:]:
+        part.finish1()
     for part in num[:2]:
         part.start6()
     for part in num[2:]:
-        part.finish1()
-    for part in num[2:]:
         part.start6()
-
+    for h in range(2):
+        total_den[DEN_ROWS[0] * h : DEN_ROWS[0] * h + DEN_ROWS[h], :] = PRIOR + den[h].finish2()
     for part in num:
         rows = slice(part.row0, part.row0 + 2 * part.half)
         coadd_ref[rows, :] = part.finish2() / total_den[rows, :]
@@ -665,7 +692,7 @@
         in_specs=[pl.BlockSpec(memory_space=pltpu.HBM)] * 9,
         out_specs=[vmem, vmem],
         out_shape=[jax.ShapeDtypeStruct((ROWS, 256), F32), jax.ShapeDtypeStruct((NEXP, 9), F32)],
-        scratch_shapes=held + fit + pieces(*DEN_ROWS) + pieces(NUM_ROWS[0] // 2, NUM_ROWS[1] // 2) * 2 + sems,
+        scratch_shapes=held + fit + pieces(*DEN_ROWS) + pieces(*NUM_PIECES[0]) + pieces(*NUM_PIECES[1]) + sems,
         compiler_params=pltpu.CompilerParams(collective_id=0, has_side_effects=True, vmem_limit_bytes=52 << 20),
         name="coadd",
     )(*(pltpu.with_memory_space_constraint(a, pltpu.HBM)

time: 99.7 us -> 96.7 us (0.970)
  Pallas kernels: 97.6 us -> 94.5 us
    pallas_call x1, Pallas kernels: 97.6 us -> 94.5 us  [per_device(): pl.pallas_call(coadd_kernel, in_specs=[pl.BlockSpec(memory_space=pltpu.HB...]
where the time goes in v5:
time: 96.7 us; the launch traced here: 96.5 us
  Pallas kernels  94.5 us (98%)
  local copies, waits for them, and re-layouts  1.39 us (1%)
    pallas_call x1, Pallas kernels, per_device(): pl.pallas_call(coadd_kernel, in_specs=[pl.BlockSpec(memory_space=pltpu.HB...  94.5 us

profile of v5, /device:TPU:0, one launch (start us, length us, event | category | flops | bytes accessed | tf_op | source)
XLA Modules:
  0.0 96.5 jit_solution(6748873004118252301)
XLA Ops:
  0.6 94.5 %coadd.1 = (f32[512,256]{1,0:T(8,128)S(1)}, f32[16,9]{1,0:T(8,128)S(1)}) custom-call(f32[1,512,4096]{2,1,0:T(8,128)} %image_hbm.1, f32[1,512,4096]{2,1,0:T(8,128)} %variance_hbm.1, s32[1,32,256]{2,1,0:T(8,128)} %mask_hbm.1, s32[16]{0:T(128)} %foot_hbm.1, s32[16,16]{1,0:T(8,128)} %owner_hbm.1, bf16[512,256]{1,0:T(8,128)(2,1)} %constant.8.clone.ch_hbm, ...), custom_call_target="tpu_custom_call" | custom-call | tf_op jit(solution)/shard_map/coadd/pallas_call | solution.py:690
  95.2 0.8 copy.13
  95.9 0.6 copy.14

commit v6 on v5

--- a/solution.py
+++ b/solution.py
@@ -25,7 +25,7 @@
 LAMBDA_REG = 0.25
 DEN_ROWS = (224, 288)
 NUM_ROWS = (224, 288)
-NUM_PIECES = ((160, 208), (64, 80))
+NUM_PIECES = ((176, 224), (48, 64))
 PRIOR = 1.0
 
 
@@ -584,7 +584,7 @@
     each(smooth, 4, 5)
     z_copies = exchange(1, gathered(0, x_copies), z, lambda k: 4 * x + lax.rem(z + k, 4))
     den[1].start3(2, 4)
-    each(smooth, 5, 8)
+    each(smooth, 5, 11)
     total = gathered(1, z_copies)
     fits = jnp.concatenate(solve_lanes(total) + [jnp.zeros((7, 128), F32)], 0)
     fits = jnp.where(used > 0.0, fits, 0.0)
@@ -627,7 +627,7 @@
         num[half].start1()
     for part in num[2:]:
         part.start1()
-    each(smooth, 8, 16)
+    each(smooth, 11, 16)
     for half in range(2):
         numerator(half, 1)
         numerator(half, 3)

time: 96.7 us -> 96.7 us (level)
  no operation moved by 1% of the time
where the time goes in v6:
time: 96.7 us; the launch traced here: 96.6 us
  Pallas kernels  94.6 us (98%)
  local copies, waits for them, and re-layouts  1.39 us (1%)
    pallas_call x1, Pallas kernels, per_device(): pl.pallas_call(coadd_kernel, in_specs=[pl.BlockSpec(memory_space=pltpu.HB...  94.6 us

profile of v6, /device:TPU:0, one launch (start us, length us, event | category | flops | bytes accessed | tf_op | source)
XLA Modules:
  0.0 96.6 jit_solution(6113916505860311658)
XLA Ops:
  0.6 94.6 %coadd.1 = (f32[512,256]{1,0:T(8,128)S(1)}, f32[16,9]{1,0:T(8,128)S(1)}) custom-call(f32[1,512,4096]{2,1,0:T(8,128)} %image_hbm.1, f32[1,512,4096]{2,1,0:T(8,128)} %variance_hbm.1, s32[1,32,256]{2,1,0:T(8,128)} %mask_hbm.1, s32[16]{0:T(128)} %foot_hbm.1, s32[16,16]{1,0:T(8,128)} %owner_hbm.1, bf16[512,256]{1,0:T(8,128)(2,1)} %constant.8.clone.ch_hbm, ...), custom_call_target="tpu_custom_call" | custom-call | tf_op jit(solution)/shard_map/coadd/pallas_call | solution.py:690
  95.2 0.8 copy.13
  96.0 0.6 copy.14

commit v7 on v5

--- a/solution.py
+++ b/solution.py
@@ -370,10 +370,7 @@
     ]
     for copy in small[:2]:
         copy.start()
-    each(lambda n, rel: load_var(n, rel).start())
-    each(lambda n, rel: load_img(n, rel).start())
-    for copy in small[2:]:
-        copy.start()
+    each(lambda n, rel: load_var(n, rel).start(), 0, 7)
 
     for copy in small[:2]:
         copy.wait()
@@ -411,6 +408,10 @@
     pl.semaphore_wait(barrier, NEXP + SKY - 2)
     for part in den:
         part.start1_chunk(2)
+    each(lambda n, rel: load_var(n, rel).start(), 7, 16)
+    each(lambda n, rel: load_img(n, rel).start())
+    for copy in small[2:]:
+        copy.start()
     halos = []
     for n, (rows, dst, to) in enumerate(((ROWS - HALO, up_ref, band + 1), (0, down_ref, band + SKY - 1))):
         copy = pltpu.make_async_remote_copy(

time: 96.7 us -> 96.7 us (level)
  no operation moved by 1% of the time
where the time goes in v7:
time: 96.7 us; the launch traced here: 96.5 us
  Pallas kernels  94.5 us (98%)
  local copies, waits for them, and re-layouts  1.39 us (1%)
    pallas_call x1, Pallas kernels, per_device(): pl.pallas_call(coadd_kernel, in_specs=[pl.BlockSpec(memory_space=pltpu.HB...  94.5 us

profile of v7, /device:TPU:0, one launch (start us, length us, event | category | flops | bytes accessed | tf_op | source)
XLA Modules:
  0.0 96.5 jit_solution(17794704714872939196)
XLA Ops:
  0.6 94.5 %coadd.1 = (f32[512,256]{1,0:T(8,128)S(1)}, f32[16,9]{1,0:T(8,128)S(1)}) custom-call(f32[1,512,4096]{2,1,0:T(8,128)} %image_hbm.1, f32[1,512,4096]{2,1,0:T(8,128)} %variance_hbm.1, s32[1,32,256]{2,1,0:T(8,128)} %mask_hbm.1, s32[16]{0:T(128)} %foot_hbm.1, s32[16,16]{1,0:T(8,128)} %owner_hbm.1, bf16[512,256]{1,0:T(8,128)(2,1)} %constant.8.clone.ch_hbm, ...), custom_call_target="tpu_custom_call" | custom-call | tf_op jit(solution)/shard_map/coadd/pallas_call | solution.py:691
  95.2 0.8 copy.13
  96.0 0.6 copy.14
